TPU v7x, 256 devices: a whole 4x4x8 slice. The times are simulated.
256 devices in a mesh: row: 32 (over y, z), col: 8 (over x, core).
Axes of the slice: x: 4, y: 4, z: 8, core: 2. Of those that a mesh axis runs over, the one named last changes fastest.
Arguments:
- blocks: bfloat16 [4096, 3, 128, 128], P(('row', 'col')), may hold values from -0.3984375 to 0.3984375
- rows: int32 [4096, 3], P(('row', 'col')), may hold values from 0 to 63, as said below
- counts: int32 [4096], P(('row', 'col')), may hold values from 1 to 3
- sketch: bfloat16 [524288, 128], P(('row', 'col')), may hold values from -6 to 6
- weights: float32 [8192], replicated, may hold values from 0.35 to 2.8
Outputs:
- basis_out: float32 [8192, 128], P(('row', 'col'))
- right_factors: bfloat16 [524288, 128], P(('row', 'col'))
Inputs may be any that keep to these rules, and one draw needn't show every extreme that they name: `rows`: the 3 entries of each document block are distinct feature blocks.
All inputs are finite; a program needn't handle non-finite values.
Results may differ from a plain program's by a relative error of at most 0.0049.
Values may be sent and summed in bfloat16 or wider, within the bound.
A program may use at most 64 MiB of HBM per device.

v0:
```python
import jax
import jax.numpy as jnp
from jax import lax
from jax.sharding import PartitionSpec as P

HIGHEST = lax.Precision.HIGHEST


def body(blocks, rows, counts, sketch, weights):
    doc_blocks = blocks.shape[0]
    slot_count = blocks.shape[1]
    block_width = blocks.shape[2]
    columns = sketch.shape[1]
    features = weights.shape[0]
    feature_blocks = features // block_width
    in_use = lax.broadcasted_iota(jnp.int32, (doc_blocks, slot_count), 1) < counts[:, None]
    segment_ids = jnp.where(in_use, rows, feature_blocks).reshape(-1)
    row_count = lax.axis_size("row")
    col_count = lax.axis_size("col")
    flat_rows = features // (row_count * col_count)
    flat_index = lax.axis_index("row") * col_count + lax.axis_index("col")
    flat_start = flat_index * flat_rows
    flat_weights = lax.dynamic_slice_in_dim(weights, flat_start, flat_rows)[:, None]
    width_now = sketch.shape[1]
    tiles_docs = sketch.reshape(doc_blocks, block_width, width_now)
    terms = jnp.einsum("dsfk,dkl->dsfl", blocks, tiles_docs, preferred_element_type=jnp.float32)
    terms = terms.reshape(doc_blocks * slot_count, block_width, width_now)
    summed = jax.ops.segment_sum(terms, segment_ids, num_segments=feature_blocks + 1)
    local_terms = summed[:feature_blocks].reshape(features, sketch.shape[1])
    flat_summed = (
        lax.psum_scatter(local_terms, ("row", "col"), scatter_dimension=0, tiled=True)
        * flat_weights
    )
    chol_factor = jnp.linalg.cholesky(
        lax.psum(jnp.dot(flat_summed.T, flat_summed, precision=HIGHEST), ("row", "col")) / features
    )
    inverse = jax.scipy.linalg.solve_triangular(
        chol_factor, jnp.eye(columns, dtype=jnp.float32), lower=True
    )
    current = jnp.dot(flat_summed, inverse.T, precision=HIGHEST)
    weighted = (current * flat_weights).astype(jnp.bfloat16)
    gathered = lax.all_gather(weighted, ("row", "col"), axis=0, tiled=True)
    width_now = gathered.shape[1]
    picked = gathered.reshape(feature_blocks, block_width, width_now)[rows]
    picked = jnp.where(in_use[:, :, None, None], picked, jnp.zeros((), gathered.dtype))
    product = jnp.einsum("dsfl,dsfk->dkl", picked, blocks, preferred_element_type=jnp.float32)
    factors = product.reshape(doc_blocks * block_width, width_now).astype(jnp.bfloat16)
    return (current, factors)


def solution(mesh):
    placed = (
        P(("row", "col"), None, None, None),
        P(("row", "col"), None),
        P(("row", "col")),
        P(("row", "col"), None),
        P(),
    )
    return jax.shard_map(
        body,
        mesh=mesh,
        in_specs=placed,
        out_specs=(P(("row", "col"), None), P(("row", "col"), None)),
        check_vma=False,
    )
```

profile of v0, /device:TPU:1, one launch (start us, length us, event | category | flops | bytes accessed | tf_op | source)
XLA Modules:
  0.0 1698.9 jit_solution(12156809714150162819)
XLA Ops:
  7.2 0.0 copy-start
  7.2 0.0 reduce-scatter.2.cloned.1.call-start
  7.2 0.8 compare_select_fusion
  8.0 0.1 copy.13
  8.1 0.1 reshape.61
  8.2 0.4 copy-done
  8.6 3.3 fusion.21
  11.9 2.5 broadcast_in_dim.27
  14.4 10.1 scatter_fusion
  24.5 4.7 slice.18
  29.1 0.0 copy-start.1
  29.1 0.0 reduce-scatter.2.cloned.1.call-update
  29.2 0.0 all-reduce.2.cloned.1.call-start
  29.2 0.8 dynamic_slice.3
  30.0 1285.4 %reduce-scatter.2.cloned.1.call-done = f32[32,128]{1,0:T(8,128)} async-done(((f32[8192,128]{1,0:T(8,128)}), f32[32,128]{1,0:T(8,128)}) %reduce-scatter.2.cloned.1.call-update) | async-done | bytes 16400 | tf_op jit(solution)/shard_map/reduce_scatter | solution.py:31
  1315.4 1.8 fusion.16
  1317.1 0.0 all-reduce.2.cloned.1.call-update
  1317.2 0.0 all-gather.2.cloned.1.call-start
  1317.2 243.8 %all-reduce.2.cloned.1.call-done = f32[128,128]{0,1:T(8,128)} async-done(((f32[128,128]{0,1:T(8,128)}), f32[128,128]{0,1:T(8,128)}) %all-reduce.2.cloned.1.call-update) | async-done | bytes 65552 | tf_op jit(solution)/shard_map/psum | solution.py:35
  1561.1 0.8 broadcast_multiply_fusion
  1561.9 0.1 copy.15
  1562.0 0.9 fusion.13
  1562.9 11.7 cholesky.17
  1574.6 0.6 compare_reduce_fusion
  1575.3 0.7 fusion.10
  1575.9 9.8 custom-call.7
  1585.7 0.2 fusion.11
  1586.0 1.6 multiply_convert_fusion
  1587.6 0.0 all-gather.2.cloned.1.call-update
  1587.6 0.1 copy.17
  1587.7 0.1 reshape.53
  1587.8 0.0 copy-done.1
  1587.8 0.1 copy.16
  1587.9 100.5 %all-gather.2.cloned.1.call-done = bf16[8192,128]{1,0:T(8,128)(2,1)} async-done(((bf16[32,128]{1,0:T(8,128)(2,1)}), bf16[8192,128]{1,0:T(8,128)(2,1)}) %all-gather.2.cloned.1.call-update) | async-done | bytes 2097168 | tf_op jit(solution)/shard_map/all_gather | solution.py:42
  1688.4 2.4 gather_fusion
  1690.9 1.5 fusion.6
  (3 shorter events, 0.0 us)
Async XLA Ops:
  7.2 1.4 copy-start
  7.2 1308.2 %reduce-scatter.2.cloned.1.call-start = ((), (), s32[]{:S(2)}) async-start(), calls=%async_computation.1 | async-start | bytes 4210688 | tf_op jit(solution)/shard_map/reduce_scatter | solution.py:31
  29.1 1558.6 %copy-start.1 = (s32[16]{0:T(128)S(1)}, s32[16]{0:T(128)}, u32[]{:S(2)}) copy-start(s32[16]{0:T(128)} %param.7) | copy-start | bytes 196
  29.2 1531.9 %all-reduce.2.cloned.1.call-start = ((), (), s32[]{:S(2)}) async-start(), calls=%async_computation.2 | async-start | bytes 131072 | tf_op jit(solution)/shard_map/psum | solution.py:35
  1317.2 371.3 %all-gather.2.cloned.1.call-start = ((), (), s32[]{:S(2)}) async-start(), calls=%async_computation.3 | async-start | bytes 2105344 | tf_op jit(solution)/shard_map/all_gather | solution.py:42
Sparse Core Ops, SparseCore 0:
  29.3 1286.0 reduce-scatter.1
  1321.4 239.5 all-reduce.1
  1587.7 100.6 all-gather.1
where the time goes:
time: 1700 us
  waiting for transfers between devices  1630 us (96%)
  other arithmetic  35.5 us (2%)
    reduce_scatter x1, waiting for transfers between devices, body(): lax.psum_scatter(local_terms, ('row', 'col'), scatter_dimension=0, tiled=...  1290 us
    psum x1, waiting for transfers between devices, body(): lax.psum(jnp.dot(flat_summed.T, flat_summed, precision=HIGHEST), ('row',...  244 us
    all_gather x1, waiting for transfers between devices, body(): gathered = lax.all_gather(weighted, ('row', 'col'), axis=0, tiled=True)  101 us
  transfers between devices with their start and end apart: 3, of which 3 were waited for; matrix products, arithmetic and copies ran while one was open for 0% of the time, Pallas kernels for 0%

commit v1 on v0

v1 whole, which is shorter than its diff:
```python
import functools

import jax
import jax.numpy as jnp
from jax import lax
from jax.experimental import pallas as pl
from jax.experimental.pallas import tpu as pltpu
from jax.sharding import PartitionSpec as P

HIGHEST = lax.Precision.HIGHEST
MESH = pl.DeviceIdType.MESH
F32, BF16 = jnp.float32, jnp.bfloat16
NX, NY, NZ, NC = 4, 4, 8, 2
HZ = NZ // 2
PIECE = 32


def terms_kernel(rows_ref, counts_ref, blocks_ref, sketch_ref, acc_ref):
    docs, slots, width = blocks_ref.shape[:3]
    zero = jnp.zeros((8, width, width), F32)

    def clear(i, carry):
        acc_ref[pl.ds(i * 8, 8)] = zero
        return carry

    lax.fori_loop(0, acc_ref.shape[0] // 8, clear, 0)
    for d in range(docs):
        product = jnp.dot(
            blocks_ref[d].reshape(slots * width, width),
            sketch_ref[d * width : (d + 1) * width, :],
            preferred_element_type=F32,
        )
        for s in range(slots):
            part = product[s * width : (s + 1) * width]
            used = s < counts_ref[d]
            acc_ref[rows_ref[d, s]] += jnp.where(used, part, jnp.zeros_like(part))


def exchange_kernel(
    p_ref, w_ref, y_ref, s_ref,
    cs, cr, xs, xr, ys, yr, zs, zr, wide,
    sem0, sem_a, sem_b, sem_z, sem_gz, sem_gb, sem_ga, sem_p,
):
    row, col = lax.axis_index("row"), lax.axis_index("col")
    x, c = lax.div(col, NC), lax.rem(col, NC)
    y, z = lax.div(row, NZ), lax.rem(row, NZ)
    partner = (row, x * NC + (1 - c))

    def shift(v, k, n):
        return lax.rem(v + k, n)

    def at(xx, yy, zz):
        return (yy * NZ + zz, xx * NC + c)

    def x_peer(k):
        return at(shift(x, k, NX), y, z)

    def y_peer(k):
        return at(x, shift(y, k, NY), z)

    def z_peer(k):
        return at(x, y, shift(z, k, NZ))

    barrier = pltpu.get_barrier_semaphore()
    greet = [partner]
    greet += [x_peer(k) for k in range(1, NX)]
    greet += [y_peer(k) for k in range(1, NY)]
    greet += [z_peer(k) for k in range(1, NZ)]
    for peer in greet:
        pl.semaphore_signal(barrier, inc=1, device_id=peer, device_id_type=MESH)

    started = []

    def send(src, dst, sems, i, peer):
        copy = pltpu.make_async_remote_copy(
            src_ref=src, dst_ref=dst, send_sem=sems.at[0, i], recv_sem=sems.at[1, i],
            device_id=peer, device_id_type=MESH,
        )
        copy.start()
        started.append(copy)
        return copy

    def piece(colour, k, i, j, core):
        if colour == 0:
            return (i, j, shift(x, k, NX), core)
        return (shift(y, k, NY), HZ + j, i, core)

    order = [(q, k) for k in (1, 2, 3, 0) for q in (0, 1)]

    def slot(q, k):
        return q * 4 + k

    for q, k in order:
        def fill(i, carry, q=q, k=k):
            for j in range(HZ):
                cs[slot(q, k), i, j] = p_ref[piece(q, k, i, j, 1 - c)].astype(BF16)
            return carry

        lax.fori_loop(0, 4, fill, 0)

    flat = row * (NX * NC) + col
    w_row = w_ref[pl.ds(lax.div(flat, 4), 1), :]
    wide[...] = jnp.broadcast_to(w_row, wide.shape).T
    pl.semaphore_wait(barrier, len(greet))

    first = {}
    for q, k in order:
        n = slot(q, k)
        first[q, k] = send(cs.at[n], cr.at[n], sem0, n, partner)
    second = {}
    for q, k in order:
        first[q, k].wait_recv()
        if k == 0:
            continue
        n = q * 3 + k - 1

        def add(i, carry, q=q, k=k, n=n):
            for j in range(HZ):
                total = p_ref[piece(q, k, i, j, c)] + cr[slot(q, k), i, j].astype(F32)
                xs[n, i, j] = total.astype(BF16)
            return carry

        lax.fori_loop(0, 4, add, 0)
        second[q, k] = send(xs.at[n], xr.at[n], sem_a, n, (x_peer if q == 0 else y_peer)(k))

    third = {}
    for q in (0, 1):
        for k in (1, 2, 3):
            second[q, k].wait_recv()
        for k in (1, 2, 3, 0):
            i = shift(y if q == 0 else x, k, 4)
            for j in range(HZ):
                total = p_ref[piece(q, 0, i, j, c)] + cr[slot(q, 0), i, j].astype(F32)
                for m in range(3):
                    total = total + xr[q * 3 + m, i, j].astype(F32)
                if k > 0:
                    ys[q * 3 + k - 1, j] = total.astype(BF16)
                else:
                    zs[q * HZ + j] = total
            if k > 0:
                n = q * 3 + k - 1
                third[q, k] = send(ys.at[n], yr.at[n], sem_b, n, (y_peer if q == 0 else x_peer)(k))

    for q in (0, 1):
        for k in (1, 2, 3):
            third[q, k].wait_recv()
        for j in range(HZ):
            total = zs[q * HZ + j]
            for m in range(3):
                total = total + yr[q * 3 + m, j].astype(F32)
            zs[q * HZ + j] = total

    fourth = [
        send(zs.at[shift(z, k, NZ)], zr.at[k - 1], sem_z, k - 1, z_peer(k)) for k in range(1, NZ)
    ]
    total = zs[z]
    for k in range(1, NZ):
        fourth[k - 1].wait_recv()
        total = total + zr[k - 1]
    w = wide[pl.ds(pl.multiple_of(lax.rem(flat, 4) * PIECE, PIECE), PIECE), :]
    summed = total * w
    s_ref[...] = summed
    y_ref[y, z, x, c] = (summed * w).astype(BF16)

    mine = y_ref.at[y, z, x, c]
    gz = [send(mine, mine, sem_gz, k - 1, z_peer(k)) for k in range(1, NZ)]
    paired = []

    def pair(part):
        paired.append(send(part, part, sem_p, len(paired), partner))

    for copy in gz:
        copy.wait_recv()
    gb = {}
    for q in (0, 1):
        part = y_ref.at[y, pl.ds(q * HZ, HZ), x, c]
        for k in (1, 2, 3):
            gb[q, k] = send(part, part, sem_gb, q * 3 + k - 1, (y_peer if q == 0 else x_peer)(k))
    pair(y_ref.at[y, :, x, c])
    ga = {}
    for q in (0, 1):
        for k in (1, 2, 3):
            gb[q, k].wait_recv()
        part = y_ref.at[:, pl.ds(0, HZ), x, c] if q == 0 else y_ref.at[y, pl.ds(HZ, HZ), :, c]
        for k in (1, 2, 3):
            ga[q, k] = send(part, part, sem_ga, q * 3 + k - 1, (x_peer if q == 0 else y_peer)(k))
        for k in (1, 2, 3):
            if q == 0:
                pair(y_ref.at[shift(y, k, NY), pl.ds(0, HZ), x, c])
            else:
                pair(y_ref.at[y, pl.ds(HZ, HZ), shift(x, k, NX), c])
    for k in (1, 3, 2):
        for q in (0, 1):
            ga[q, k].wait_recv()
            if q == 0:
                pair(y_ref.at[:, pl.ds(0, HZ), shift(x, NX - k, NX), c])
            else:
                pair(y_ref.at[shift(y, NY - k, NY), pl.ds(HZ, HZ), :, c])
    for copy in paired:
        copy.wait_recv()
    for copy in started:
        copy.wait_send()


def gram_kernel(rows_ref, counts_ref, y_ref, blocks_ref, w_ref, g_ref, t_ref, turned):
    docs, slots, width = blocks_ref.shape[:3]
    features = y_ref.shape[0] * width

    def one(f, carry):
        tile = y_ref[f]
        across = tile.astype(F32).T
        turned[f] = across.astype(BF16)
        w = w_ref[pl.ds(f, 1), :]
        scaled = (across * (1.0 / (w * w))).astype(BF16)
        return carry + jnp.dot(scaled, tile, preferred_element_type=F32)

    gram = lax.fori_loop(0, y_ref.shape[0], one, jnp.zeros((width, width), F32))
    g_ref[...] = gram / features
    for d in range(docs):
        total = jnp.zeros((width, width), F32)
        for s in range(slots):
            part = turned[rows_ref[d, s]]
            part = jnp.where(s < counts_ref[d], part, jnp.zeros_like(part))
            total = total + jnp.dot(part, blocks_ref[d, s], preferred_element_type=F32)
        t_ref[d] = total


def split(a):
    high = a.astype(BF16)
    return high, (a - high.astype(F32)).astype(BF16)


def finish_kernel(t_ref, inverse_ref, s_ref, basis_ref, factors_ref):
    docs, width = t_ref.shape[:2]
    inverse = inverse_ref[...]
    basis_ref[...] = lax.dot_general(
        s_ref[...], inverse, (((1,), (1,)), ((), ())), precision=HIGHEST, preferred_element_type=F32
    )
    high, low = split(inverse)
    for d in range(docs):
        t_high, t_low = split(t_ref[d])
        out = jnp.dot(high, t_high, preferred_element_type=F32)
        out = out + jnp.dot(high, t_low, preferred_element_type=F32)
        out = out + jnp.dot(low, t_high, preferred_element_type=F32)
        factors_ref[d * width : (d + 1) * width, :] = out.T.astype(BF16)


def vmem():
    return pl.BlockSpec(memory_space=pltpu.VMEM)


def smem():
    return pl.BlockSpec(memory_space=pltpu.SMEM)


def body(blocks, rows, counts, sketch, weights):
    docs, slots, width = blocks.shape[:3]
    features = weights.shape[0]
    feature_blocks = features // width
    columns = sketch.shape[1]
    square = (width, columns)
    params = functools.partial(pltpu.CompilerParams, vmem_limit_bytes=24 << 20)
    terms = pl.pallas_call(
        terms_kernel,
        name="terms",
        out_shape=jax.ShapeDtypeStruct((feature_blocks,) + square, F32),
        in_specs=[smem(), smem(), vmem(), vmem()],
        out_specs=vmem(),
        compiler_params=params(),
    )(rows, counts, blocks, sketch)
    w = weights.reshape(feature_blocks, width)
    grid = (NY, NZ, NX, NC, PIECE, columns)
    tail = (PIECE, columns)
    dma = pltpu.SemaphoreType.DMA
    gathered, summed = pl.pallas_call(
        exchange_kernel,
        name="exchange",
        out_shape=(jax.ShapeDtypeStruct(grid, BF16), jax.ShapeDtypeStruct(tail, F32)),
        in_specs=[vmem(), vmem()],
        out_specs=(vmem(), vmem()),
        scratch_shapes=[
            pltpu.VMEM((8, 4, HZ) + tail, BF16), pltpu.VMEM((8, 4, HZ) + tail, BF16),
            pltpu.VMEM((6, 4, HZ) + tail, BF16), pltpu.VMEM((6, 4, HZ) + tail, BF16),
            pltpu.VMEM((6, HZ) + tail, BF16), pltpu.VMEM((6, HZ) + tail, BF16),
            pltpu.VMEM((NZ,) + tail, F32), pltpu.VMEM((NZ - 1,) + tail, F32),
            pltpu.VMEM(square, F32),
            dma((2, 8)), dma((2, 6)), dma((2, 6)), dma((2, NZ - 1)),
            dma((2, NZ - 1)), dma((2, 6)), dma((2, 6)), dma((2, 13)),
        ],
        compiler_params=params(collective_id=0, has_side_effects=True),
    )(terms.reshape(grid), w)
    gram, turned = pl.pallas_call(
        gram_kernel,
        name="gram",
        out_shape=(jax.ShapeDtypeStruct(square, F32), jax.ShapeDtypeStruct((docs,) + square, F32)),
        in_specs=[smem(), smem(), vmem(), vmem(), vmem()],
        out_specs=(vmem(), vmem()),
        scratch_shapes=[pltpu.VMEM((feature_blocks,) + square, BF16)],
        compiler_params=params(),
    )(rows, counts, gathered.reshape((feature_blocks,) + square), blocks, w)
    chol_factor = jnp.linalg.cholesky(gram, symmetrize_input=False)
    inverse = jax.scipy.linalg.solve_triangular(
        chol_factor, jnp.eye(columns, dtype=F32), lower=True
    )
    return pl.pallas_call(
        finish_kernel,
        name="finish",
        out_shape=(
            jax.ShapeDtypeStruct(tail, F32),
            jax.ShapeDtypeStruct((docs * width, columns), BF16),
        ),
        in_specs=[vmem(), vmem(), vmem()],
        out_specs=(vmem(), vmem()),
        compiler_params=params(),
    )(turned, inverse, summed)


def solution(mesh):
    placed = (
        P(("row", "col"), None, None, None),
        P(("row", "col"), None),
        P(("row", "col")),
        P(("row", "col"), None),
        P(),
    )
    return jax.shard_map(
        body,
        mesh=mesh,
        in_specs=placed,
        out_specs=(P(("row", "col"), None), P(("row", "col"), None)),
        check_vma=False,
    )
```

time: 1700 us -> 95.3 us (0.06)
  waiting for transfers between devices: 1630 us -> 0 us
  Pallas kernels: 0 us -> 67.4 us
    reduce_scatter x1 -> x0, waiting for transfers between devices: 1290 us -> none  [body(): lax.psum_scatter(local_terms, ('row', 'col'), scatter_dimension=0, tiled=...]
    psum x1 -> x0, waiting for transfers between devices: 244 us -> none  [body(): lax.psum(jnp.dot(flat_summed.T, flat_summed, precision=HIGHEST), ('row',...]
    all_gather x1 -> x0, waiting for transfers between devices: 101 us -> none  [body(): gathered = lax.all_gather(weighted, ('row', 'col'), axis=0, tiled=True)]
    pallas_call x0 -> x4, Pallas kernels: none -> 67.4 us  [the longest x1 49.1 us: body(): pl.pallas_call(exchange_kernel, name='exchange', out_shape=(jax.ShapeDtyp...]
  transfers between devices with their start and end apart: 3 -> 0, of which waited for: 3 -> 0; matrix products, arithmetic and copies ran while one was open for 0% -> 0% of each run, Pallas kernels for 0% -> 0%
where the time goes in v1:
time: 95.3 us; the launch traced here: 95.1 us
  Pallas kernels  67.4 us (71%)
  other arithmetic  22.9 us (24%)
  local copies, waits for them, and re-layouts  3.87 us (4%)
    pallas_call x1, Pallas kernels, body(): pl.pallas_call(exchange_kernel, name='exchange', out_shape=(jax.ShapeDtyp...  49.1 us
    pallas_call x1, Pallas kernels, body(): pl.pallas_call(gram_kernel, name='gram', out_shape=(jax.ShapeDtypeStruct(...  15.3 us
    another operation x3, other arithmetic, body(): chol_factor = jnp.linalg.cholesky(gram, symmetrize_input=False)  12.4 us
    another operation x2, other arithmetic, body(): jax.scipy.linalg.solve_triangular(chol_factor, jnp.eye(columns, dtype=F32...  10.5 us
    unnamed x9, local copies, waits for them, and re-layouts  3.87 us

profile of v1, /device:TPU:1, one launch (start us, length us, event | category | flops | bytes accessed | tf_op | source)
XLA Modules:
  0.0 95.1 jit_solution(15555194355823642997)
XLA Ops:
  0.6 0.8 copy.8.rows_ref
  1.4 0.0 copy-start
  1.4 1.4 %copy-done = bf16[16,3,128,128]{3,2,1,0:T(8,128)(2,1)S(1)} copy-done((bf16[16,3,128,128]{3,2,1,0:T(8,128)(2,1)S(1)}, bf16[16,3,128,128]{3,2,1,0:T(8,128)(2,1)}, u32[]{:S(2)}) %copy-start) | copy-done | bytes 1572888
  2.8 0.0 copy-start.1
  2.8 1.0 %copy-done.1 = bf16[2048,128]{1,0:T(8,128)(2,1)S(1)} copy-done((bf16[2048,128]{1,0:T(8,128)(2,1)S(1)}, bf16[2048,128]{1,0:T(8,128)(2,1)}, u32[]{:S(2)}) %copy-start.1) | copy-done | bytes 524312
  3.8 0.0 copy-start.3
  3.8 0.7 copy-done.3
  4.5 0.0 copy-start.2
  4.5 1.5 %terms.1 = f32[64,128,128]{2,1,0:T(8,128)S(1)} custom-call(s32[16,3]{1,0:T(8,128)S(1)} %copy.8.rows_ref, s32[16]{0:T(128)S(1)} %copy-done.3, bf16[16,3,128,128]{3,2,1,0:T(8,128)(2,1)S(1)} %copy-done, bf16[2048,128]{1,0:T(8,128)(2,1)S(1)} %copy-done.1), custom_call_target="tpu_custom_call" | custom-call | tf_op jit(solution)/shard_map/terms/pallas_call | solution.py:263
  6.0 0.0 copy-done.2
  6.0 49.1 %exchange.1 = (bf16[4,8,4,2,32,128]{5,4,3,2,1,0:T(8,128)(2,1)S(1)}, f32[32,128]{1,0:T(8,128)S(1)}) custom-call(f32[4,8,4,2,32,128]{5,4,3,2,1,0:T(8,128)S(1)} %bitcast.8, f32[64,128]{1,0:T(8,128)S(1)} %bitcast.10), custom_call_target="tpu_custom_call" | custom-call | tf_op jit(solution)/shard_map/exchange/pallas_call | solution.py:275
  55.1 15.3 %gram.1 = (f32[128,128]{1,0:T(8,128)S(1)}, f32[16,128,128]{2,1,0:T(8,128)S(1)}) custom-call(s32[16,3]{1,0:T(8,128)S(1)} %copy.8.rows_ref, s32[16]{0:T(128)S(1)} %copy-done.3, bf16[64,128,128]{2,1,0:T(8,128)(2,1)S(1)} %bitcast.9, bf16[16,3,128,128]{3,2,1,0:T(8,128)(2,1)S(1)} %copy-done, f32[64,128]{1,0:T(8,128)S(1)} %bitcast.11), custom_call_target="tpu_custom_call" | custom-call | tf_op jit(solution)/shard_map/gram/pallas_call | solution.py:292
  70.4 11.7 %cholesky.17 = f32[128,128]{1,0:T(8,128)S(1)} custom-call(f32[128,128]{1,0:T(8,128)S(1)} %get-tuple-element.8), custom_call_target="Cholesky" | custom-call | tf_op jit(solution)/shard_map/jit(cholesky)/cholesky | solution.py:301
  82.2 0.6 compare_reduce_fusion
  82.8 0.7 fusion
  83.5 9.8 %custom-call.7 = f32[1,128,128]{1,2,0:T(8,128)S(1)} custom-call(f32[1,128,128]{2,1,0:T(8,128)S(1)} %fusion), custom_call_target="InvertDiagBlocksLowerTriangular" | custom-call | tf_op jit(solution)/shard_map/jit(_solve_triangular)/triangular_solve | solution.py:302
  93.3 0.2 fusion.1.inverse_ref
  93.5 1.5 %finish.1 = (f32[32,128]{1,0:T(8,128)}, bf16[2048,128]{1,0:T(8,128)(2,1)}) custom-call(f32[16,128,128]{2,1,0:T(8,128)S(1)} %get-tuple-element.7.t_ref, f32[128,128]{1,0:T(8,128)S(1)} %fusion.1.inverse_ref, f32[32,128]{1,0:T(8,128)S(1)} %get-tuple-element.9.s_ref), custom_call_target="tpu_custom_call" | custom-call | tf_op jit(solution)/shard_map/finish/pallas_call | solution.py:305
  (1 shorter events, 0.0 us)
Async XLA Ops:
  1.4 1.4 %copy-start = (bf16[16,3,128,128]{3,2,1,0:T(8,128)(2,1)S(1)}, bf16[16,3,128,128]{3,2,1,0:T(8,128)(2,1)}, u32[]{:S(2)}) copy-start(bf16[16,3,128,128]{3,2,1,0:T(8,128)(2,1)} %blocks_ref.3) | copy-start | bytes 4718596
  2.8 1.0 %copy-start.1 = (bf16[2048,128]{1,0:T(8,128)(2,1)S(1)}, bf16[2048,128]{1,0:T(8,128)(2,1)}, u32[]{:S(2)}) copy-start(bf16[2048,128]{1,0:T(8,128)(2,1)} %sketch_ref.1) | copy-start | bytes 1572868
  3.8 0.7 copy-start.3
  4.5 1.5 %copy-start.2 = (f32[8192]{0:T(1024)S(1)}, f32[8192]{0:T(1024)}, u32[]{:S(2)}) copy-start(f32[8192]{0:T(1024)} %param.9) | copy-start | bytes 98308

commit v2 on v1

--- a/solution.py
+++ b/solution.py
@@ -15,8 +15,30 @@
 PIECE = 32
 
 
-def terms_kernel(rows_ref, counts_ref, blocks_ref, sketch_ref, acc_ref):
-    docs, slots, width = blocks_ref.shape[:3]
+def scalars(rows_hbm, counts_hbm, rows_ref, counts_ref, sems):
+    copies = [
+        pltpu.make_async_copy(rows_hbm, rows_ref, sems.at[0]),
+        pltpu.make_async_copy(counts_hbm, counts_ref, sems.at[1]),
+    ]
+    for copy in copies:
+        copy.start()
+    return copies
+
+
+def terms_kernel(
+    rows_hbm, counts_hbm, blocks_ref, sketch_ref, acc_ref,
+    held, docs_held, sems, rows_ref, counts_ref, sem_i,
+):
+    docs, slots, width = held.shape[:3]
+    step = 4
+    indices = scalars(rows_hbm, counts_hbm, rows_ref, counts_ref, sem_i)
+    copies = []
+    for i in range(docs // step):
+        a = pltpu.make_async_copy(sketch_ref.at[pl.ds(i * step * width, step * width)], docs_held.at[pl.ds(i * step * width, step * width)], sems.at[0, i])
+        c = pltpu.make_async_copy(blocks_ref.at[pl.ds(i * step, step)], held.at[pl.ds(i * step, step)], sems.at[1, i])
+        a.start()
+        c.start()
+        copies.append((a, c))
     zero = jnp.zeros((8, width, width), F32)
 
     def clear(i, carry):
@@ -24,16 +46,21 @@
         return carry
 
     lax.fori_loop(0, acc_ref.shape[0] // 8, clear, 0)
+    for copy in indices:
+        copy.wait()
     for d in range(docs):
+        if d % step == 0:
+            for copy in copies[d // step]:
+                copy.wait()
         product = jnp.dot(
-            blocks_ref[d].reshape(slots * width, width),
-            sketch_ref[d * width : (d + 1) * width, :],
+            held[d].reshape(slots * width, width),
+            docs_held[d * width : (d + 1) * width, :],
             preferred_element_type=F32,
         )
         for s in range(slots):
             part = product[s * width : (s + 1) * width]
             used = s < counts_ref[d]
-            acc_ref[rows_ref[d, s]] += jnp.where(used, part, jnp.zeros_like(part))
+            acc_ref[rows_ref[s, d]] += jnp.where(used, part, jnp.zeros_like(part))
 
 
 def exchange_kernel(
@@ -202,46 +229,109 @@
         copy.wait_send()
 
 
-def gram_kernel(rows_ref, counts_ref, y_ref, blocks_ref, w_ref, g_ref, t_ref, turned):
-    docs, slots, width = blocks_ref.shape[:3]
-    features = y_ref.shape[0] * width
-
-    def one(f, carry):
-        tile = y_ref[f]
-        across = tile.astype(F32).T
-        turned[f] = across.astype(BF16)
-        w = w_ref[pl.ds(f, 1), :]
-        scaled = (across * (1.0 / (w * w))).astype(BF16)
-        return carry + jnp.dot(scaled, tile, preferred_element_type=F32)
-
-    gram = lax.fori_loop(0, y_ref.shape[0], one, jnp.zeros((width, width), F32))
-    g_ref[...] = gram / features
-    for d in range(docs):
-        total = jnp.zeros((width, width), F32)
-        for s in range(slots):
-            part = turned[rows_ref[d, s]]
-            part = jnp.where(s < counts_ref[d], part, jnp.zeros_like(part))
-            total = total + jnp.dot(part, blocks_ref[d, s], preferred_element_type=F32)
-        t_ref[d] = total
-
-
 def split(a):
     high = a.astype(BF16)
     return high, (a - high.astype(F32)).astype(BF16)
 
 
-def finish_kernel(t_ref, inverse_ref, s_ref, basis_ref, factors_ref):
-    docs, width = t_ref.shape[:2]
-    inverse = inverse_ref[...]
+def factor(m_ref, linv_ref, b):
+    n = m_ref.shape[0]
+    lane = lax.broadcasted_iota(jnp.int32, (b, n), 1)
+    sub = lax.broadcasted_iota(jnp.int32, (b, n), 0)
+    for r0 in range(0, n, b):
+        panel = m_ref[r0 : r0 + b, :]
+        cols = jnp.stack([jnp.broadcast_to(panel[:, r0 + j : r0 + j + 1], (b, n)) for j in range(b)])
+        inside = (lane >= r0) & (lane < r0 + b)
+        panel = jnp.where(inside, (lane - r0 == sub).astype(F32), panel)
+        pivots = jnp.ones((b, n), F32)
+        for k in range(b):
+            base = (k // 8) * 8
+            col = cols[0]
+            pivot = col[k - base : k - base + 1]
+            pivots = jnp.where(sub == k, pivot, pivots)
+            if k == b - 1:
+                break
+            inv = 1.0 / pivot
+            col = jnp.where(sub[base:] > k, col, 0.0)
+            row = panel[k : k + 1] * inv
+            lower = panel[base:] - col * row
+            panel = lower if base == 0 else jnp.concatenate([panel[:base], lower], axis=0)
+            rest = cols[1:]
+            cols = rest - col[None] * (rest[:, k - base : k - base + 1, :] * inv)
+            if (k + 1) % 8 == 0:
+                cols = cols[:, 8:]
+        scaled = panel * lax.rsqrt(pivots)
+        linv_ref[r0 : r0 + b, :] = jnp.where(lane < r0 + b, scaled, 0.0)
+        if r0 + b < n:
+            h = scaled.astype(BF16)
+            rem = scaled - h.astype(F32)
+            m = rem.astype(BF16)
+            l = (rem - m.astype(F32)).astype(BF16)
+            right = lane >= r0 + b
+            zero = jnp.zeros_like(h)
+            hf, mf, lf = (jnp.where(right, v.astype(F32), 0.0).astype(BF16) for v in (h, m, l))
+            left = jnp.concatenate([hf, hf, mf, mf, hf, lf], axis=0)
+            rightm = jnp.concatenate([h, m, h, m, l, h], axis=0)
+            update = lax.dot_general(left, rightm, (((0,), (0,)), ((), ())), preferred_element_type=F32)
+            rest = m_ref[r0 + b :, :]
+            lane2 = lax.broadcasted_iota(jnp.int32, rest.shape, 1)
+            rest = jnp.where((lane2 >= r0) & (lane2 < r0 + b), 0.0, rest)
+            m_ref[r0 + b :, :] = rest - update[r0 + b :, :]
+
+
+def tail_kernel(
+    rows_hbm, counts_hbm, y_ref, blocks_ref, w_ref, s_ref, basis_ref, factors_ref,
+    turned, m_ref, linv_ref, t_ref, held, sem, rows_ref, counts_ref, sem_i,
+):
+    slots, docs = rows_ref.shape
+    indices = scalars(rows_hbm, counts_hbm, rows_ref, counts_ref, sem_i)
+    width = y_ref.shape[1]
+    count = y_ref.shape[0]
+    features = count * width
+    copy = pltpu.make_async_copy(blocks_ref, held, sem)
+    copy.start()
+    group = 8
+
+    def some(i, carry):
+        scaled = []
+        for j in range(group):
+            f = i * group + j
+            tile = y_ref[f]
+            across = tile.T
+            turned[f] = across
+            w = w_ref[pl.ds(f, 1), :]
+            scaled.append((across.astype(F32) * (1.0 / (w * w))).astype(BF16))
+        left = jnp.concatenate(scaled, axis=1)
+        right = y_ref[pl.ds(i * group, group)].reshape(group * width, width)
+        return carry + jnp.dot(left, right, preferred_element_type=F32)
+
+    gram = lax.fori_loop(0, count // group, some, jnp.zeros((width, width), F32))
+    m_ref[...] = gram / features
+    copy.wait()
+    for copy in indices:
+        copy.wait()
+
+    def product(d):
+        parts = []
+        for s in range(slots):
+            part = turned[rows_ref[s, d]]
+            parts.append(jnp.where(s < counts_ref[d], part, jnp.zeros_like(part)))
+        left = jnp.concatenate(parts, axis=1)
+        right = held[d].reshape(slots * width, width)
+        t_ref[d] = jnp.dot(left, right, preferred_element_type=F32)
+
+    for d in range(docs):
+        product(d)
+    factor(m_ref, linv_ref, 16)
+    inverse = linv_ref[...]
     basis_ref[...] = lax.dot_general(
         s_ref[...], inverse, (((1,), (1,)), ((), ())), precision=HIGHEST, preferred_element_type=F32
     )
     high, low = split(inverse)
+    both = jnp.concatenate([high, high, low], axis=1)
     for d in range(docs):
         t_high, t_low = split(t_ref[d])
-        out = jnp.dot(high, t_high, preferred_element_type=F32)
-        out = out + jnp.dot(high, t_low, preferred_element_type=F32)
-        out = out + jnp.dot(low, t_high, preferred_element_type=F32)
+        out = jnp.dot(both, jnp.concatenate([t_high, t_low, t_high], axis=0), preferred_element_type=F32)
         factors_ref[d * width : (d + 1) * width, :] = out.T.astype(BF16)
 
 
@@ -249,8 +339,8 @@
     return pl.BlockSpec(memory_space=pltpu.VMEM)
 
 
-def smem():
-    return pl.BlockSpec(memory_space=pltpu.SMEM)
+def hbm():
+    return pl.BlockSpec(memory_space=pltpu.HBM)
 
 
 def body(blocks, rows, counts, sketch, weights):
@@ -259,19 +349,27 @@
     feature_blocks = features // width
     columns = sketch.shape[1]
     square = (width, columns)
+    tail = (PIECE, columns)
+    dma = pltpu.SemaphoreType.DMA
     params = functools.partial(pltpu.CompilerParams, vmem_limit_bytes=24 << 20)
+    rows = rows.T
+    rows, counts, blocks, sketch = (
+        pltpu.with_memory_space_constraint(a, pltpu.HBM) for a in (rows, counts, blocks, sketch)
+    )
     terms = pl.pallas_call(
         terms_kernel,
         name="terms",
         out_shape=jax.ShapeDtypeStruct((feature_blocks,) + square, F32),
-        in_specs=[smem(), smem(), vmem(), vmem()],
+        in_specs=[hbm()] * 4,
         out_specs=vmem(),
+        scratch_shapes=[
+            pltpu.VMEM(blocks.shape, BF16), pltpu.VMEM(sketch.shape, BF16), dma((2, 4)),
+            pltpu.SMEM(rows.shape, jnp.int32), pltpu.SMEM(counts.shape, jnp.int32), dma((2,)),
+        ],
         compiler_params=params(),
     )(rows, counts, blocks, sketch)
     w = weights.reshape(feature_blocks, width)
     grid = (NY, NZ, NX, NC, PIECE, columns)
-    tail = (PIECE, columns)
-    dma = pltpu.SemaphoreType.DMA
     gathered, summed = pl.pallas_call(
         exchange_kernel,
         name="exchange",
@@ -289,30 +387,24 @@
         ],
         compiler_params=params(collective_id=0, has_side_effects=True),
     )(terms.reshape(grid), w)
-    gram, turned = pl.pallas_call(
-        gram_kernel,
-        name="gram",
-        out_shape=(jax.ShapeDtypeStruct(square, F32), jax.ShapeDtypeStruct((docs,) + square, F32)),
-        in_specs=[smem(), smem(), vmem(), vmem(), vmem()],
-        out_specs=(vmem(), vmem()),
-        scratch_shapes=[pltpu.VMEM((feature_blocks,) + square, BF16)],
-        compiler_params=params(),
-    )(rows, counts, gathered.reshape((feature_blocks,) + square), blocks, w)
-    chol_factor = jnp.linalg.cholesky(gram, symmetrize_input=False)
-    inverse = jax.scipy.linalg.solve_triangular(
-        chol_factor, jnp.eye(columns, dtype=F32), lower=True
-    )
     return pl.pallas_call(
-        finish_kernel,
-        name="finish",
+        tail_kernel,
+        name="tail",
         out_shape=(
             jax.ShapeDtypeStruct(tail, F32),
             jax.ShapeDtypeStruct((docs * width, columns), BF16),
         ),
-        in_specs=[vmem(), vmem(), vmem()],
+        in_specs=[hbm(), hbm(), vmem(), hbm(), vmem(), vmem()],
         out_specs=(vmem(), vmem()),
+        scratch_shapes=[
+            pltpu.VMEM((feature_blocks,) + square, BF16),
+            pltpu.VMEM(square, F32), pltpu.VMEM(square, F32),
+            pltpu.VMEM((docs,) + square, F32),
+            pltpu.VMEM(blocks.shape, BF16), dma(()),
+            pltpu.SMEM(rows.shape, jnp.int32), pltpu.SMEM(counts.shape, jnp.int32), dma((2,)),
+        ],
         compiler_params=params(),
-    )(turned, inverse, summed)
+    )(rows, counts, gathered.reshape((feature_blocks,) + square), blocks, w, summed)
 
 
 def solution(mesh):

time: 95.3 us -> 59.2 us (0.62)
  other arithmetic: 22.9 us -> 0 us
  Pallas kernels: 67.4 us -> 58.5 us
  local copies, waits for them, and re-layouts: 3.87 us -> 0.01 us
    another operation x5 -> x0, other arithmetic: 22.9 us -> none  [the longest x3 12.4 us: body(): chol_factor = jnp.linalg.cholesky(gram, symmetrize_input=False)]
    pallas_call x2 -> x1, Pallas kernels: 16.8 us -> 7.16 us  [body(): pl.pallas_call(tail_kernel, name='tail', out_shape=(jax.ShapeDtypeStruct(...]
    unnamed x9 -> x2, local copies, waits for them, and re-layouts: 3.87 us -> 0.01 us
where the time goes in v2:
time: 59.2 us; the launch traced here: 59.1 us
  Pallas kernels  58.5 us (99%)
  between operations  0.66 us (1%)
    pallas_call x1, Pallas kernels, body(): pl.pallas_call(exchange_kernel, name='exchange', out_shape=(jax.ShapeDtyp...  49.1 us
    pallas_call x1, Pallas kernels, body(): pl.pallas_call(tail_kernel, name='tail', out_shape=(jax.ShapeDtypeStruct(...  7.16 us
    pallas_call x1, Pallas kernels, body(): pl.pallas_call(terms_kernel, name='terms', out_shape=jax.ShapeDtypeStruct...  2.25 us

profile of v2, /device:TPU:1, one launch (start us, length us, event | category | flops | bytes accessed | tf_op | source)
XLA Modules:
  0.0 59.1 jit_solution(2581509602500887036)
XLA Ops:
  0.6 0.0 copy-start
  0.6 2.3 %terms.1 = f32[64,128,128]{2,1,0:T(8,128)S(1)} custom-call(s32[3,16]{1,0:T(4,128)} %bitcast.8, s32[16]{0:T(128)} %counts_hbm.3, bf16[16,3,128,128]{3,2,1,0:T(8,128)(2,1)} %blocks_ref.3, bf16[2048,128]{1,0:T(8,128)(2,1)} %sketch_ref.1), custom_call_target="tpu_custom_call" | custom-call | tf_op jit(solution)/shard_map/terms/pallas_call | solution.py:359
  2.9 0.0 copy-done
  2.9 49.1 %exchange.1 = (bf16[4,8,4,2,32,128]{5,4,3,2,1,0:T(8,128)(2,1)S(1)}, f32[32,128]{1,0:T(8,128)S(1)}) custom-call(f32[4,8,4,2,32,128]{5,4,3,2,1,0:T(8,128)S(1)} %bitcast.4, f32[64,128]{1,0:T(8,128)S(1)} %bitcast.6), custom_call_target="tpu_custom_call" | custom-call | tf_op jit(solution)/shard_map/exchange/pallas_call | solution.py:373
  52.0 7.2 %tail.1 = (f32[32,128]{1,0:T(8,128)}, bf16[2048,128]{1,0:T(8,128)(2,1)}) custom-call(s32[3,16]{1,0:T(4,128)} %bitcast.9, s32[16]{0:T(128)} %counts_hbm.3, bf16[64,128,128]{2,1,0:T(8,128)(2,1)S(1)} %bitcast.5, bf16[16,3,128,128]{3,2,1,0:T(8,128)(2,1)} %blocks_ref.3, f32[64,128]{1,0:T(8,128)S(1)} %bitcast.7, f32[32,128]{1,0:T(8,128)S(1)} %get-tuple-element.5.s_ref), custom_call_target="tpu_custom_call" | custom-call | tf_op jit(solution)/shard_map/tail/pallas_call | solution.py:390
Async XLA Ops:
  0.6 2.3 %copy-start = (f32[8192]{0:T(1024)S(1)}, f32[8192]{0:T(1024)}, u32[]{:S(2)}) copy-start(f32[8192]{0:T(1024)} %param.9) | copy-start | bytes 98308

commit v3 on v2

--- a/solution.py
+++ b/solution.py
@@ -11,7 +11,7 @@
 MESH = pl.DeviceIdType.MESH
 F32, BF16 = jnp.float32, jnp.bfloat16
 NX, NY, NZ, NC = 4, 4, 8, 2
-HZ = NZ // 2
+QZ = 2
 PIECE = 32
 
 
@@ -79,48 +79,44 @@
     def at(xx, yy, zz):
         return (yy * NZ + zz, xx * NC + c)
 
-    def x_peer(k):
-        return at(shift(x, k, NX), y, z)
-
-    def y_peer(k):
-        return at(x, shift(y, k, NY), z)
-
-    def z_peer(k):
-        return at(x, y, shift(z, k, NZ))
-
+    x_peer = [at(shift(x, k, NX), y, z) for k in range(NX)]
+    y_peer = [at(x, shift(y, k, NY), z) for k in range(NY)]
+    z_peer = [at(x, y, shift(z, k, NZ)) for k in range(NZ)]
+    greet = [partner] + z_peer[1:] + x_peer[1:] + y_peer[1:]
     barrier = pltpu.get_barrier_semaphore()
-    greet = [partner]
-    greet += [x_peer(k) for k in range(1, NX)]
-    greet += [y_peer(k) for k in range(1, NY)]
-    greet += [z_peer(k) for k in range(1, NZ)]
     for peer in greet:
         pl.semaphore_signal(barrier, inc=1, device_id=peer, device_id_type=MESH)
 
+    streams = range(NZ // QZ)
+    a_peer = [(x_peer, y_peer)[s % 2] for s in streams]
+    b_peer = [(y_peer, x_peer)[s % 2] for s in streams]
+    a_at = [(x, y)[s % 2] for s in streams]
+    b_at = [(y, x)[s % 2] for s in streams]
     started = []
 
-    def send(src, dst, sems, i, peer):
-        copy = pltpu.make_async_remote_copy(
-            src_ref=src, dst_ref=dst, send_sem=sems.at[0, i], recv_sem=sems.at[1, i],
+    def copy_to(src, dst, send_sem, recv_sem, peer):
+        return pltpu.make_async_remote_copy(
+            src_ref=src, dst_ref=dst, send_sem=send_sem, recv_sem=recv_sem,
             device_id=peer, device_id_type=MESH,
         )
+
+    def send(src, dst, sems, i, peer):
+        copy = copy_to(src, dst, sems.at[0, i], sems.at[1, i], peer)
         copy.start()
         started.append(copy)
         return copy
 
-    def piece(colour, k, i, j, core):
-        if colour == 0:
-            return (i, j, shift(x, k, NX), core)
-        return (shift(y, k, NY), HZ + j, i, core)
-
-    order = [(q, k) for k in (1, 2, 3, 0) for q in (0, 1)]
-
-    def slot(q, k):
-        return q * 4 + k
-
-    for q, k in order:
-        def fill(i, carry, q=q, k=k):
-            for j in range(HZ):
-                cs[slot(q, k), i, j] = p_ref[piece(q, k, i, j, 1 - c)].astype(BF16)
+    def piece(s, k, b, j, core):
+        a = shift(a_at[s], k, 4)
+        if s % 2 == 0:
+            return (b, s * QZ + j, a, core)
+        return (a, s * QZ + j, b, core)
+
+    order = [(s, k) for s0 in (0, 2) for k in (2, 1, 3, 0) for s in (s0, s0 + 1)]
+    for s, k in order:
+        def fill(b, carry, s=s, k=k):
+            for j in range(QZ):
+                cs[s * 4 + k, b, j] = p_ref[piece(s, k, b, j, 1 - c)].astype(BF16)
             return carry
 
         lax.fori_loop(0, 4, fill, 0)
@@ -130,103 +126,117 @@
     wide[...] = jnp.broadcast_to(w_row, wide.shape).T
     pl.semaphore_wait(barrier, len(greet))
 
-    first = {}
-    for q, k in order:
-        n = slot(q, k)
-        first[q, k] = send(cs.at[n], cr.at[n], sem0, n, partner)
-    second = {}
-    for q, k in order:
-        first[q, k].wait_recv()
+    first, second, third = {}, {}, {}
+    for s, k in order:
+        n = s * 4 + k
+        first[s, k] = send(cs.at[n], cr.at[n], sem0, n, partner)
+    for s, k in order:
+        first[s, k].wait_recv()
         if k == 0:
             continue
-        n = q * 3 + k - 1
-
-        def add(i, carry, q=q, k=k, n=n):
-            for j in range(HZ):
-                total = p_ref[piece(q, k, i, j, c)] + cr[slot(q, k), i, j].astype(F32)
-                xs[n, i, j] = total.astype(BF16)
+        n = s * 3 + k - 1
+
+        def add(b, carry, s=s, k=k, n=n):
+            for j in range(QZ):
+                total = p_ref[piece(s, k, b, j, c)] + cr[s * 4 + k, b, j].astype(F32)
+                xs[n, b, j] = total.astype(BF16)
             return carry
 
         lax.fori_loop(0, 4, add, 0)
-        second[q, k] = send(xs.at[n], xr.at[n], sem_a, n, (x_peer if q == 0 else y_peer)(k))
-
-    third = {}
-    for q in (0, 1):
-        for k in (1, 2, 3):
-            second[q, k].wait_recv()
-        for k in (1, 2, 3, 0):
-            i = shift(y if q == 0 else x, k, 4)
-            for j in range(HZ):
-                total = p_ref[piece(q, 0, i, j, c)] + cr[slot(q, 0), i, j].astype(F32)
+        second[s, k] = send(xs.at[n], xr.at[n], sem_a, n, a_peer[s][k])
+
+    for s in streams:
+        for k in (1, 3, 2):
+            second[s, k].wait_recv()
+        for k in (2, 1, 3, 0):
+            b = shift(b_at[s], k, 4)
+            for j in range(QZ):
+                total = p_ref[piece(s, 0, b, j, c)] + cr[s * 4, b, j].astype(F32)
                 for m in range(3):
-                    total = total + xr[q * 3 + m, i, j].astype(F32)
+                    total = total + xr[s * 3 + m, b, j].astype(F32)
                 if k > 0:
-                    ys[q * 3 + k - 1, j] = total.astype(BF16)
+                    ys[s * 3 + k - 1, j] = total.astype(BF16)
                 else:
-                    zs[q * HZ + j] = total
+                    zs[s * QZ + j] = total
             if k > 0:
-                n = q * 3 + k - 1
-                third[q, k] = send(ys.at[n], yr.at[n], sem_b, n, (y_peer if q == 0 else x_peer)(k))
-
-    for q in (0, 1):
-        for k in (1, 2, 3):
-            third[q, k].wait_recv()
-        for j in range(HZ):
-            total = zs[q * HZ + j]
+                n = s * 3 + k - 1
+                third[s, k] = send(ys.at[n], yr.at[n], sem_b, n, b_peer[s][k])
+
+    def fourth(there):
+        return copy_to(
+            zs.at[there], zr.at[z], sem_z.at[0, there], sem_z.at[1, z], at(x, y, there)
+        )
+
+    def arrival(k):
+        here = shift(z, k, NZ)
+        return copy_to(zs.at[here], zr.at[here], sem_z.at[0, here], sem_z.at[1, here], z_peer[k])
+
+    for s in streams:
+        for k in (1, 3, 2):
+            third[s, k].wait_recv()
+        for j in range(QZ):
+            total = zs[s * QZ + j]
             for m in range(3):
-                total = total + yr[q * 3 + m, j].astype(F32)
-            zs[q * HZ + j] = total
-
-    fourth = [
-        send(zs.at[shift(z, k, NZ)], zr.at[k - 1], sem_z, k - 1, z_peer(k)) for k in range(1, NZ)
-    ]
+                total = total + yr[s * 3 + m, j].astype(F32)
+            zs[s * QZ + j] = total
+        for j in range(QZ):
+            there = s * QZ + j
+
+            @pl.when(z != there)
+            def _(there=there):
+                fourth(there).start()
+
     total = zs[z]
-    for k in range(1, NZ):
-        fourth[k - 1].wait_recv()
-        total = total + zr[k - 1]
+    for k in (1, 7, 2, 6, 3, 5, 4):
+        arrival(k).wait_recv()
+        total = total + zr[shift(z, k, NZ)]
     w = wide[pl.ds(pl.multiple_of(lax.rem(flat, 4) * PIECE, PIECE), PIECE), :]
     summed = total * w
     s_ref[...] = summed
-    y_ref[y, z, x, c] = (summed * w).astype(BF16)
-
-    mine = y_ref.at[y, z, x, c]
-    gz = [send(mine, mine, sem_gz, k - 1, z_peer(k)) for k in range(1, NZ)]
-    paired = []
+
+    mine_s, odd = lax.div(z, QZ), lax.rem(lax.div(z, QZ), 2)
+    mine_a, mine_b = x + odd * (y - x), y + odd * (x - y)
+    y_ref[mine_s, c, mine_a, mine_b, lax.rem(z, QZ)] = (summed * w).astype(BF16)
+    mine = y_ref.at[mine_s, c, mine_a, mine_b, lax.rem(z, QZ)]
+    for k in (4, 3, 5, 2, 6, 1, 7):
+        copy = copy_to(mine, mine, sem_gz.at[0, k], sem_gz.at[1, z], z_peer[k])
+        copy.start()
+        started.append(copy)
+    gb, ga, paired = {}, {}, []
 
     def pair(part):
         paired.append(send(part, part, sem_p, len(paired), partner))
 
-    for copy in gz:
-        copy.wait_recv()
-    gb = {}
-    for q in (0, 1):
-        part = y_ref.at[y, pl.ds(q * HZ, HZ), x, c]
-        for k in (1, 2, 3):
-            gb[q, k] = send(part, part, sem_gb, q * 3 + k - 1, (y_peer if q == 0 else x_peer)(k))
-    pair(y_ref.at[y, :, x, c])
-    ga = {}
-    for q in (0, 1):
-        for k in (1, 2, 3):
-            gb[q, k].wait_recv()
-        part = y_ref.at[:, pl.ds(0, HZ), x, c] if q == 0 else y_ref.at[y, pl.ds(HZ, HZ), :, c]
-        for k in (1, 2, 3):
-            ga[q, k] = send(part, part, sem_ga, q * 3 + k - 1, (x_peer if q == 0 else y_peer)(k))
-        for k in (1, 2, 3):
-            if q == 0:
-                pair(y_ref.at[shift(y, k, NY), pl.ds(0, HZ), x, c])
-            else:
-                pair(y_ref.at[y, pl.ds(HZ, HZ), shift(x, k, NX), c])
-    for k in (1, 3, 2):
-        for q in (0, 1):
-            ga[q, k].wait_recv()
-            if q == 0:
-                pair(y_ref.at[:, pl.ds(0, HZ), shift(x, NX - k, NX), c])
-            else:
-                pair(y_ref.at[shift(y, NY - k, NY), pl.ds(HZ, HZ), :, c])
+    for s in streams:
+        part = y_ref.at[s, c, a_at[s], b_at[s]]
+        for j in range(QZ):
+            there = s * QZ + j
+
+            @pl.when(z != there)
+            def _(there=there, j=j, part=part):
+                copy_to(
+                    part.at[j], part.at[j], sem_gz.at[0, 0], sem_gz.at[1, there], at(x, y, there)
+                ).wait_recv()
+
+        for k in (2, 1, 3):
+            gb[s, k] = send(part, part, sem_gb, s * 3 + k - 1, b_peer[s][k])
+    for s in streams:
+        for k in (1, 3, 2):
+            gb[s, k].wait_recv()
+        part = y_ref.at[s, c, a_at[s]]
+        for k in (2, 1, 3):
+            ga[s, k] = send(part, part, sem_ga, s * 3 + k - 1, a_peer[s][k])
+        pair(part)
+    for s in streams:
+        for k in (1, 3, 2):
+            ga[s, k].wait_recv()
+            pair(y_ref.at[s, c, shift(a_at[s], 4 - k, 4)])
     for copy in paired:
         copy.wait_recv()
     for copy in started:
         copy.wait_send()
+    for k in range(1, NZ):
+        arrival(k).wait_send()
 
 
 def split(a):
@@ -285,24 +295,29 @@
 ):
     slots, docs = rows_ref.shape
     indices = scalars(rows_hbm, counts_hbm, rows_ref, counts_ref, sem_i)
-    width = y_ref.shape[1]
-    count = y_ref.shape[0]
+    count, width = w_ref.shape
     features = count * width
     copy = pltpu.make_async_copy(blocks_ref, held, sem)
     copy.start()
     group = 8
 
     def some(i, carry):
-        scaled = []
+        scaled, tiles = [], []
         for j in range(group):
             f = i * group + j
-            tile = y_ref[f]
+            s, odd = lax.rem(i, 2) * 2 + j // 4, (j // 4) % 2
+            tile = []
+            for m in range(4):
+                ax = (lax.div(i, 2), 2 * (j % 2) + m // 2)
+                tile.append(y_ref[s, m % 2, ax[1 - odd], ax[odd], (j // 2) % 2])
+            tile = jnp.concatenate(tile, axis=0)
+            tiles.append(tile)
             across = tile.T
             turned[f] = across
             w = w_ref[pl.ds(f, 1), :]
             scaled.append((across.astype(F32) * (1.0 / (w * w))).astype(BF16))
         left = jnp.concatenate(scaled, axis=1)
-        right = y_ref[pl.ds(i * group, group)].reshape(group * width, width)
+        right = jnp.concatenate(tiles, axis=0)
         return carry + jnp.dot(left, right, preferred_element_type=F32)
 
     gram = lax.fori_loop(0, count // group, some, jnp.zeros((width, width), F32))
@@ -370,20 +385,21 @@
     )(rows, counts, blocks, sketch)
     w = weights.reshape(feature_blocks, width)
     grid = (NY, NZ, NX, NC, PIECE, columns)
+    streamed = (NZ // QZ, NC, 4, 4, QZ, PIECE, columns)
     gathered, summed = pl.pallas_call(
         exchange_kernel,
         name="exchange",
-        out_shape=(jax.ShapeDtypeStruct(grid, BF16), jax.ShapeDtypeStruct(tail, F32)),
+        out_shape=(jax.ShapeDtypeStruct(streamed, BF16), jax.ShapeDtypeStruct(tail, F32)),
         in_specs=[vmem(), vmem()],
         out_specs=(vmem(), vmem()),
         scratch_shapes=[
-            pltpu.VMEM((8, 4, HZ) + tail, BF16), pltpu.VMEM((8, 4, HZ) + tail, BF16),
-            pltpu.VMEM((6, 4, HZ) + tail, BF16), pltpu.VMEM((6, 4, HZ) + tail, BF16),
-            pltpu.VMEM((6, HZ) + tail, BF16), pltpu.VMEM((6, HZ) + tail, BF16),
-            pltpu.VMEM((NZ,) + tail, F32), pltpu.VMEM((NZ - 1,) + tail, F32),
+            pltpu.VMEM((16, 4, QZ) + tail, BF16), pltpu.VMEM((16, 4, QZ) + tail, BF16),
+            pltpu.VMEM((12, 4, QZ) + tail, BF16), pltpu.VMEM((12, 4, QZ) + tail, BF16),
+            pltpu.VMEM((12, QZ) + tail, BF16), pltpu.VMEM((12, QZ) + tail, BF16),
+            pltpu.VMEM((NZ,) + tail, F32), pltpu.VMEM((NZ,) + tail, F32),
             pltpu.VMEM(square, F32),
-            dma((2, 8)), dma((2, 6)), dma((2, 6)), dma((2, NZ - 1)),
-            dma((2, NZ - 1)), dma((2, 6)), dma((2, 6)), dma((2, 13)),
+            dma((2, 16)), dma((2, 12)), dma((2, 12)), dma((2, NZ)),
+            dma((2, NZ)), dma((2, 12)), dma((2, 12)), dma((2, 16)),
         ],
         compiler_params=params(collective_id=0, has_side_effects=True),
     )(terms.reshape(grid), w)
@@ -404,7 +420,7 @@
             pltpu.SMEM(rows.shape, jnp.int32), pltpu.SMEM(counts.shape, jnp.int32), dma((2,)),
         ],
         compiler_params=params(),
-    )(rows, counts, gathered.reshape((feature_blocks,) + square), blocks, w, summed)
+    )(rows, counts, gathered, blocks, w, summed)
 
 
 def solution(mesh):

time: 59.2 us -> 56.6 us (0.956)
  Pallas kernels: 58.5 us -> 55.8 us
    pallas_call x1, Pallas kernels: 49.1 us -> 46.4 us  [body(): pl.pallas_call(exchange_kernel, name='exchange', out_shape=(jax.ShapeDtyp...]
where the time goes in v3:
time: 56.6 us; the launch traced here: 56.5 us
  Pallas kernels  55.8 us (99%)
  between operations  0.66 us (1%)
    pallas_call x1, Pallas kernels, body(): pl.pallas_call(exchange_kernel, name='exchange', out_shape=(jax.ShapeDtyp...  46.4 us
    pallas_call x1, Pallas kernels, body(): pl.pallas_call(tail_kernel, name='tail', out_shape=(jax.ShapeDtypeStruct(...  7.17 us
    pallas_call x1, Pallas kernels, body(): pl.pallas_call(terms_kernel, name='terms', out_shape=jax.ShapeDtypeStruct...  2.25 us

profile of v3, /device:TPU:1, one launch (start us, length us, event | category | flops | bytes accessed | tf_op | source)
XLA Modules:
  0.0 56.5 jit_solution(5560684413559264330)
XLA Ops:
  0.6 0.0 copy-start
  0.6 2.3 %terms.1 = f32[64,128,128]{2,1,0:T(8,128)S(1)} custom-call(s32[3,16]{1,0:T(4,128)} %bitcast.6, s32[16]{0:T(128)} %counts_hbm.3, bf16[16,3,128,128]{3,2,1,0:T(8,128)(2,1)} %blocks_ref.3, bf16[2048,128]{1,0:T(8,128)(2,1)} %sketch_ref.1), custom_call_target="tpu_custom_call" | custom-call | tf_op jit(solution)/shard_map/terms/pallas_call | solution.py:374
  2.9 0.0 copy-done
  2.9 46.4 %exchange.1 = (bf16[4,2,4,4,2,32,128]{6,5,4,3,2,1,0:T(8,128)(2,1)S(1)}, f32[32,128]{1,0:T(8,128)S(1)}) custom-call(f32[4,8,4,2,32,128]{5,4,3,2,1,0:T(8,128)S(1)} %bitcast.3, f32[64,128]{1,0:T(8,128)S(1)} %bitcast.4), custom_call_target="tpu_custom_call" | custom-call | tf_op jit(solution)/shard_map/exchange/pallas_call | solution.py:389
  49.3 7.2 %tail.1 = (f32[32,128]{1,0:T(8,128)}, bf16[2048,128]{1,0:T(8,128)(2,1)}) custom-call(s32[3,16]{1,0:T(4,128)} %bitcast.7, s32[16]{0:T(128)} %counts_hbm.3, bf16[4,2,4,4,2,32,128]{6,5,4,3,2,1,0:T(8,128)(2,1)S(1)} %get-tuple-element.4.y_ref, bf16[16,3,128,128]{3,2,1,0:T(8,128)(2,1)} %blocks_ref.3, f32[64,128]{1,0:T(8,128)S(1)} %bitcast.5, ...), custom_call_target="tpu_custom_call" | custom-call | tf_op jit(solution)/shard_map/tail/pallas_call | solution.py:406
Async XLA Ops:
  0.6 2.3 %copy-start = (f32[8192]{0:T(1024)S(1)}, f32[8192]{0:T(1024)}, u32[]{:S(2)}) copy-start(f32[8192]{0:T(1024)} %param.9) | copy-start | bytes 98308

commit v4 on v3

--- a/solution.py
+++ b/solution.py
@@ -64,8 +64,8 @@
 
 
 def exchange_kernel(
-    p_ref, w_ref, y_ref, s_ref,
-    cs, cr, xs, xr, ys, yr, zs, zr, wide,
+    p_ref, w_ref, blocks_ref, y_ref, s_ref, g_ref, bt_ref,
+    held, sem_h, iw_ref, cs, cr, xs, xr, ys, yr, zs, zr, wide,
     sem0, sem_a, sem_b, sem_z, sem_gz, sem_gb, sem_ga, sem_p,
 ):
     row, col = lax.axis_index("row"), lax.axis_index("col")
@@ -87,6 +87,9 @@
     for peer in greet:
         pl.semaphore_signal(barrier, inc=1, device_id=peer, device_id_type=MESH)
 
+    load = pltpu.make_async_copy(blocks_ref, held, sem_h)
+    load.start()
+
     streams = range(NZ // QZ)
     a_peer = [(x_peer, y_peer)[s % 2] for s in streams]
     b_peer = [(y_peer, x_peer)[s % 2] for s in streams]
@@ -111,6 +114,38 @@
         if s % 2 == 0:
             return (b, s * QZ + j, a, core)
         return (a, s * QZ + j, b, core)
+
+    def inverse_weights(first, last):
+        def some(i, carry):
+            for j in range(8):
+                w = w_ref[pl.ds(i * 8 + j, 1), :]
+                turned = jnp.broadcast_to(1.0 / (w * w), wide.shape).T
+                s, odd = lax.rem(i, 2) * 2 + j // 4, (j // 4) % 2
+                for m in range(4):
+                    ax = (lax.div(i, 2), 2 * (j % 2) + m // 2)
+                    rows = turned[m * PIECE : (m + 1) * PIECE]
+                    iw_ref[s, m % 2, ax[1 - odd], ax[odd], (j // 2) % 2] = rows
+            return carry
+
+        lax.fori_loop(first, last, some, 0)
+
+    def turn_tiles(first, last):
+        def some(i, carry):
+            for j in range(4):
+                d = i * 4 + j
+                parts = [held[d, m].T for m in range(held.shape[1])]
+                bt_ref[d] = jnp.concatenate(parts, axis=1)
+            return carry
+
+        lax.fori_loop(first, last, some, 0)
+
+    def add_gram(s, core):
+        tall = (4 * 4 * QZ * PIECE, wide.shape[1])
+        part = y_ref[s, core].reshape(tall)
+        scaled = (part.astype(F32) * iw_ref[s, core].reshape(tall)).astype(BF16)
+        g_ref[...] += lax.dot_general(
+            scaled, part, (((0,), (0,)), ((), ())), preferred_element_type=F32
+        )
 
     order = [(s, k) for s0 in (0, 2) for k in (2, 1, 3, 0) for s in (s0, s0 + 1)]
     for s, k in order:
@@ -145,6 +180,7 @@
         lax.fori_loop(0, 4, add, 0)
         second[s, k] = send(xs.at[n], xr.at[n], sem_a, n, a_peer[s][k])
 
+    inverse_weights(0, 2)
     for s in streams:
         for k in (1, 3, 2):
             second[s, k].wait_recv()
@@ -186,6 +222,7 @@
             def _(there=there):
                 fourth(there).start()
 
+    inverse_weights(2, 6)
     total = zs[z]
     for k in (1, 7, 2, 6, 3, 5, 4):
         arrival(k).wait_recv()
@@ -203,6 +240,10 @@
         copy.start()
         started.append(copy)
     gb, ga, paired = {}, {}, []
+    inverse_weights(6, 8)
+    load.wait()
+    turn_tiles(0, 4)
+    g_ref[...] = jnp.zeros_like(g_ref)
 
     def pair(part):
         paired.append(send(part, part, sem_p, len(paired), partner))
@@ -231,8 +272,13 @@
         for k in (1, 3, 2):
             ga[s, k].wait_recv()
             pair(y_ref.at[s, c, shift(a_at[s], 4 - k, 4)])
-    for copy in paired:
-        copy.wait_recv()
+        if s > 0:
+            add_gram(s - 1, c)
+    add_gram(streams[-1], c)
+    for s in streams:
+        for copy in [paired[s]] + paired[4 + 3 * s : 7 + 3 * s]:
+            copy.wait_recv()
+        add_gram(s, 1 - c)
     for copy in started:
         copy.wait_send()
     for k in range(1, NZ):
@@ -246,43 +292,63 @@
 
 def factor(m_ref, linv_ref, b):
     n = m_ref.shape[0]
+    whole = m_ref[...]
+    on_diagonal = lax.broadcasted_iota(jnp.int32, (n, n), 0) == lax.broadcasted_iota(
+        jnp.int32, (n, n), 1
+    )
+    diagonal = jnp.where(on_diagonal, whole, 0.0)
+    across = lax.rsqrt(jnp.sum(diagonal, axis=0, keepdims=True))
+    down = lax.rsqrt(jnp.sum(diagonal, axis=1, keepdims=True))
+    m_ref[...] = whole * down * across
     lane = lax.broadcasted_iota(jnp.int32, (b, n), 1)
     sub = lax.broadcasted_iota(jnp.int32, (b, n), 0)
     for r0 in range(0, n, b):
         panel = m_ref[r0 : r0 + b, :]
-        cols = jnp.stack([jnp.broadcast_to(panel[:, r0 + j : r0 + j + 1], (b, n)) for j in range(b)])
+        cols = jnp.stack(
+            [jnp.broadcast_to(panel[:, r0 + j : r0 + j + 1], (b, n)) for j in range(b)]
+        )
         inside = (lane >= r0) & (lane < r0 + b)
         panel = jnp.where(inside, (lane - r0 == sub).astype(F32), panel)
         pivots = jnp.ones((b, n), F32)
-        for k in range(b):
+        for k in range(0, b, 2):
             base = (k // 8) * 8
-            col = cols[0]
-            pivot = col[k - base : k - base + 1]
-            pivots = jnp.where(sub == k, pivot, pivots)
-            if k == b - 1:
-                break
-            inv = 1.0 / pivot
-            col = jnp.where(sub[base:] > k, col, 0.0)
-            row = panel[k : k + 1] * inv
-            lower = panel[base:] - col * row
+            i = k - base
+            c0, c1 = cols[0], cols[1]
+            p, q, r = c0[i : i + 1], c1[i : i + 1], c1[i + 1 : i + 2]
+            det = p * r - q * q
+            over_p, over_det = 1.0 / p, 1.0 / det
+            pivots = jnp.where(sub == k, p, jnp.where(sub == k + 1, det * over_p, pivots))
+            below = sub[base:]
+            alpha = jnp.where(
+                below > k + 1,
+                (r * c0 - q * c1) * over_det,
+                jnp.where(below == k + 1, q * over_p, 0.0),
+            )
+            beta = jnp.where(below > k + 1, (p * c1 - q * c0) * over_det, 0.0)
+            lower = panel[base:] - (alpha * panel[k : k + 1] + beta * panel[k + 1 : k + 2])
             panel = lower if base == 0 else jnp.concatenate([panel[:base], lower], axis=0)
-            rest = cols[1:]
-            cols = rest - col[None] * (rest[:, k - base : k - base + 1, :] * inv)
-            if (k + 1) % 8 == 0:
-                cols = cols[:, 8:]
+            if k + 2 < b:
+                rest = cols[2:]
+                cols = rest - (
+                    alpha[None] * rest[:, i : i + 1, :] + beta[None] * rest[:, i + 1 : i + 2, :]
+                )
+                if (k + 2) % 8 == 0:
+                    cols = cols[:, 8:]
         scaled = panel * lax.rsqrt(pivots)
-        linv_ref[r0 : r0 + b, :] = jnp.where(lane < r0 + b, scaled, 0.0)
+        linv_ref[r0 : r0 + b, :] = jnp.where(lane < r0 + b, scaled * across, 0.0)
         if r0 + b < n:
             h = scaled.astype(BF16)
             rem = scaled - h.astype(F32)
             m = rem.astype(BF16)
             l = (rem - m.astype(F32)).astype(BF16)
             right = lane >= r0 + b
-            zero = jnp.zeros_like(h)
             hf, mf, lf = (jnp.where(right, v.astype(F32), 0.0).astype(BF16) for v in (h, m, l))
-            left = jnp.concatenate([hf, hf, mf, mf, hf, lf], axis=0)
-            rightm = jnp.concatenate([h, m, h, m, l, h], axis=0)
-            update = lax.dot_general(left, rightm, (((0,), (0,)), ((), ())), preferred_element_type=F32)
+            update = lax.dot_general(
+                jnp.concatenate([hf, hf, mf, mf, hf, lf], axis=0),
+                jnp.concatenate([h, m, h, m, l, h], axis=0),
+                (((0,), (0,)), ((), ())),
+                preferred_element_type=F32,
+            )
             rest = m_ref[r0 + b :, :]
             lane2 = lax.broadcasted_iota(jnp.int32, rest.shape, 1)
             rest = jnp.where((lane2 >= r0) & (lane2 < r0 + b), 0.0, rest)
@@ -290,53 +356,35 @@
 
 
 def tail_kernel(
-    rows_hbm, counts_hbm, y_ref, blocks_ref, w_ref, s_ref, basis_ref, factors_ref,
-    turned, m_ref, linv_ref, t_ref, held, sem, rows_ref, counts_ref, sem_i,
+    rows_hbm, counts_hbm, y_ref, bt_ref, g_ref, s_ref, basis_ref, factors_ref,
+    m_ref, linv_ref, t_ref, rows_ref, counts_ref, sem_i,
 ):
     slots, docs = rows_ref.shape
+    width = g_ref.shape[0]
+    features = y_ref.size // width
     indices = scalars(rows_hbm, counts_hbm, rows_ref, counts_ref, sem_i)
-    count, width = w_ref.shape
-    features = count * width
-    copy = pltpu.make_async_copy(blocks_ref, held, sem)
-    copy.start()
-    group = 8
-
-    def some(i, carry):
-        scaled, tiles = [], []
-        for j in range(group):
-            f = i * group + j
-            s, odd = lax.rem(i, 2) * 2 + j // 4, (j // 4) % 2
-            tile = []
-            for m in range(4):
-                ax = (lax.div(i, 2), 2 * (j % 2) + m // 2)
-                tile.append(y_ref[s, m % 2, ax[1 - odd], ax[odd], (j // 2) % 2])
-            tile = jnp.concatenate(tile, axis=0)
-            tiles.append(tile)
-            across = tile.T
-            turned[f] = across
-            w = w_ref[pl.ds(f, 1), :]
-            scaled.append((across.astype(F32) * (1.0 / (w * w))).astype(BF16))
-        left = jnp.concatenate(scaled, axis=1)
-        right = jnp.concatenate(tiles, axis=0)
-        return carry + jnp.dot(left, right, preferred_element_type=F32)
-
-    gram = lax.fori_loop(0, count // group, some, jnp.zeros((width, width), F32))
-    m_ref[...] = gram / features
-    copy.wait()
+    m_ref[...] = g_ref[...] * (1.0 / features)
     for copy in indices:
         copy.wait()
 
-    def product(d):
+    def tile(f):
+        row = lax.div(f, 2)
+        y, z = lax.div(row, NZ), lax.rem(row, NZ)
+        s = lax.div(z, QZ)
+        odd = lax.rem(s, 2)
+        parts = []
+        for m in range(4):
+            x = lax.rem(f, 2) * 2 + m // 2
+            a, b = x + odd * (y - x), y + odd * (x - y)
+            parts.append(y_ref[s, m % 2, a, b, lax.rem(z, QZ)])
+        return jnp.concatenate(parts, axis=0)
+
+    for d in range(docs):
         parts = []
         for s in range(slots):
-            part = turned[rows_ref[s, d]]
+            part = tile(rows_ref[s, d])
             parts.append(jnp.where(s < counts_ref[d], part, jnp.zeros_like(part)))
-        left = jnp.concatenate(parts, axis=1)
-        right = held[d].reshape(slots * width, width)
-        t_ref[d] = jnp.dot(left, right, preferred_element_type=F32)
-
-    for d in range(docs):
-        product(d)
+        t_ref[d] = jnp.dot(bt_ref[d], jnp.concatenate(parts, axis=0), preferred_element_type=F32)
     factor(m_ref, linv_ref, 16)
     inverse = linv_ref[...]
     basis_ref[...] = lax.dot_general(
@@ -346,8 +394,11 @@
     both = jnp.concatenate([high, high, low], axis=1)
     for d in range(docs):
         t_high, t_low = split(t_ref[d])
-        out = jnp.dot(both, jnp.concatenate([t_high, t_low, t_high], axis=0), preferred_element_type=F32)
-        factors_ref[d * width : (d + 1) * width, :] = out.T.astype(BF16)
+        out = lax.dot_general(
+            jnp.concatenate([t_high, t_low, t_high], axis=1), both,
+            (((1,), (1,)), ((), ())), preferred_element_type=F32,
+        )
+        factors_ref[d * width : (d + 1) * width, :] = out.astype(BF16)
 
 
 def vmem():
@@ -386,13 +437,18 @@
     w = weights.reshape(feature_blocks, width)
     grid = (NY, NZ, NX, NC, PIECE, columns)
     streamed = (NZ // QZ, NC, 4, 4, QZ, PIECE, columns)
-    gathered, summed = pl.pallas_call(
+    gathered, summed, gram, turned = pl.pallas_call(
         exchange_kernel,
         name="exchange",
-        out_shape=(jax.ShapeDtypeStruct(streamed, BF16), jax.ShapeDtypeStruct(tail, F32)),
-        in_specs=[vmem(), vmem()],
-        out_specs=(vmem(), vmem()),
+        out_shape=(
+            jax.ShapeDtypeStruct(streamed, BF16), jax.ShapeDtypeStruct(tail, F32),
+            jax.ShapeDtypeStruct(square, F32),
+            jax.ShapeDtypeStruct((docs, width, slots * width), BF16),
+        ),
+        in_specs=[vmem(), vmem(), hbm()],
+        out_specs=(vmem(), vmem(), vmem(), vmem()),
         scratch_shapes=[
+            pltpu.VMEM(blocks.shape, BF16), dma(()), pltpu.VMEM(streamed, F32),
             pltpu.VMEM((16, 4, QZ) + tail, BF16), pltpu.VMEM((16, 4, QZ) + tail, BF16),
             pltpu.VMEM((12, 4, QZ) + tail, BF16), pltpu.VMEM((12, 4, QZ) + tail, BF16),
             pltpu.VMEM((12, QZ) + tail, BF16), pltpu.VMEM((12, QZ) + tail, BF16),
@@ -402,7 +458,7 @@
             dma((2, NZ)), dma((2, 12)), dma((2, 12)), dma((2, 16)),
         ],
         compiler_params=params(collective_id=0, has_side_effects=True),
-    )(terms.reshape(grid), w)
+    )(terms.reshape(grid), w, blocks)
     return pl.pallas_call(
         tail_kernel,
         name="tail",
@@ -410,17 +466,15 @@
             jax.ShapeDtypeStruct(tail, F32),
             jax.ShapeDtypeStruct((docs * width, columns), BF16),
         ),
-        in_specs=[hbm(), hbm(), vmem(), hbm(), vmem(), vmem()],
+        in_specs=[hbm(), hbm(), vmem(), vmem(), vmem(), vmem()],
         out_specs=(vmem(), vmem()),
         scratch_shapes=[
-            pltpu.VMEM((feature_blocks,) + square, BF16),
             pltpu.VMEM(square, F32), pltpu.VMEM(square, F32),
             pltpu.VMEM((docs,) + square, F32),
-            pltpu.VMEM(blocks.shape, BF16), dma(()),
             pltpu.SMEM(rows.shape, jnp.int32), pltpu.SMEM(counts.shape, jnp.int32), dma((2,)),
         ],
         compiler_params=params(),
-    )(rows, counts, gathered, blocks, w, summed)
+    )(rows, counts, gathered, turned, gram, summed)
 
 
 def solution(mesh):

time: 56.6 us -> 55.9 us (0.988)
  Pallas kernels: 55.8 us -> 55.1 us
    pallas_call x1, Pallas kernels: 7.17 us -> 6.12 us  [body(): pl.pallas_call(tail_kernel, name='tail', out_shape=(jax.ShapeDtypeStruct(...]
where the time goes in v4:
time: 55.9 us; the launch traced here: 55.7 us
  Pallas kernels  55.1 us (99%)
  between operations  0.66 us (1%)
    pallas_call x1, Pallas kernels, body(): pl.pallas_call(exchange_kernel, name='exchange', out_shape=(jax.ShapeDtyp...  46.7 us
    pallas_call x1, Pallas kernels, body(): pl.pallas_call(tail_kernel, name='tail', out_shape=(jax.ShapeDtypeStruct(...  6.12 us
    pallas_call x1, Pallas kernels, body(): pl.pallas_call(terms_kernel, name='terms', out_shape=jax.ShapeDtypeStruct...  2.25 us

profile of v4, /device:TPU:1, one launch (start us, length us, event | category | flops | bytes accessed | tf_op | source)
XLA Modules:
  0.0 55.7 jit_solution(6530338654330686220)
XLA Ops:
  0.6 0.0 copy-start
  0.6 2.3 %terms.1 = f32[64,128,128]{2,1,0:T(8,128)S(1)} custom-call(s32[3,16]{1,0:T(4,128)} %bitcast.5, s32[16]{0:T(128)} %counts_hbm.3, bf16[16,3,128,128]{3,2,1,0:T(8,128)(2,1)} %blocks_ref.3, bf16[2048,128]{1,0:T(8,128)(2,1)} %sketch_ref.1), custom_call_target="tpu_custom_call" | custom-call | tf_op jit(solution)/shard_map/terms/pallas_call | solution.py:425
  2.9 0.0 copy-done
  2.9 46.7 %exchange.1 = (bf16[4,2,4,4,2,32,128]{6,5,4,3,2,1,0:T(8,128)(2,1)S(1)}, f32[32,128]{1,0:T(8,128)S(1)}, f32[128,128]{1,0:T(8,128)S(1)}, bf16[16,128,384]{2,1,0:T(8,128)(2,1)S(1)}) custom-call(f32[4,8,4,2,32,128]{5,4,3,2,1,0:T(8,128)S(1)} %bitcast.3, f32[64,128]{1,0:T(8,128)S(1)} %bitcast.4, bf16[16,3,128,128]{3,2,1,0:T(8,128)(2,1)} %blocks_ref.3), custom_call_target="tpu_custom_call" | custom-call | tf_op jit(solution)/shard_map/exchange/pallas_call | solution.py:440
  49.6 6.1 %tail.1 = (f32[32,128]{1,0:T(8,128)}, bf16[2048,128]{1,0:T(8,128)(2,1)}) custom-call(s32[3,16]{1,0:T(4,128)} %bitcast.6, s32[16]{0:T(128)} %counts_hbm.3, bf16[4,2,4,4,2,32,128]{6,5,4,3,2,1,0:T(8,128)(2,1)S(1)} %get-tuple-element.6.y_ref, bf16[16,128,384]{2,1,0:T(8,128)(2,1)S(1)} %get-tuple-element.7.bt_ref, f32[128,128]{1,0:T(8,128)S(1)} %get-tuple-element.8.g_ref, ...), custom_call_target="tpu_custom_call" | custom-call | tf_op jit(solution)/shard_map/tail/pallas_call | solution.py:462
Async XLA Ops:
  0.6 2.3 %copy-start = (f32[8192]{0:T(1024)S(1)}, f32[8192]{0:T(1024)}, u32[]{:S(2)}) copy-start(f32[8192]{0:T(1024)} %param.9) | copy-start | bytes 98308

commit v5 on v4

--- a/solution.py
+++ b/solution.py
@@ -13,6 +13,7 @@
 NX, NY, NZ, NC = 4, 4, 8, 2
 QZ = 2
 PIECE = 32
+PANEL = 16
 
 
 def scalars(rows_hbm, counts_hbm, rows_ref, counts_ref, sems):
@@ -82,7 +83,8 @@
     x_peer = [at(shift(x, k, NX), y, z) for k in range(NX)]
     y_peer = [at(x, shift(y, k, NY), z) for k in range(NY)]
     z_peer = [at(x, y, shift(z, k, NZ)) for k in range(NZ)]
-    greet = [partner] + z_peer[1:] + x_peer[1:] + y_peer[1:]
+    greet = [z_peer[k] for k in (4, 3, 5, 2, 6)] + [x_peer[2], y_peer[2]]
+    greet += [z_peer[1], z_peer[7], x_peer[1], x_peer[3], y_peer[1], y_peer[3], partner]
     barrier = pltpu.get_barrier_semaphore()
     for peer in greet:
         pl.semaphore_signal(barrier, inc=1, device_id=peer, device_id_type=MESH)
@@ -268,17 +270,22 @@
         for k in (2, 1, 3):
             ga[s, k] = send(part, part, sem_ga, s * 3 + k - 1, a_peer[s][k])
         pair(part)
+    def add_partner(s):
+        for copy in [paired[s]] + paired[4 + 3 * s : 7 + 3 * s]:
+            copy.wait_recv()
+        add_gram(s, 1 - c)
+
     for s in streams:
         for k in (1, 3, 2):
             ga[s, k].wait_recv()
             pair(y_ref.at[s, c, shift(a_at[s], 4 - k, 4)])
         if s > 0:
             add_gram(s - 1, c)
+        if s > 1:
+            add_partner(s - 2)
     add_gram(streams[-1], c)
-    for s in streams:
-        for copy in [paired[s]] + paired[4 + 3 * s : 7 + 3 * s]:
-            copy.wait_recv()
-        add_gram(s, 1 - c)
+    for s in streams[-2:]:
+        add_partner(s)
     for copy in started:
         copy.wait_send()
     for k in range(1, NZ):
@@ -290,7 +297,7 @@
     return high, (a - high.astype(F32)).astype(BF16)
 
 
-def factor(m_ref, linv_ref, b):
+def factor(m_ref, linv_ref, b, between):
     n = m_ref.shape[0]
     whole = m_ref[...]
     on_diagonal = lax.broadcasted_iota(jnp.int32, (n, n), 0) == lax.broadcasted_iota(
@@ -353,19 +360,18 @@
             lane2 = lax.broadcasted_iota(jnp.int32, rest.shape, 1)
             rest = jnp.where((lane2 >= r0) & (lane2 < r0 + b), 0.0, rest)
             m_ref[r0 + b :, :] = rest - update[r0 + b :, :]
+        between(r0 // b)
 
 
 def tail_kernel(
     rows_hbm, counts_hbm, y_ref, bt_ref, g_ref, s_ref, basis_ref, factors_ref,
-    m_ref, linv_ref, t_ref, rows_ref, counts_ref, sem_i,
+    m_ref, linv_ref, t_ref, f_ref, b_ref, sem_o, rows_ref, counts_ref, sem_i,
 ):
     slots, docs = rows_ref.shape
     width = g_ref.shape[0]
     features = y_ref.size // width
     indices = scalars(rows_hbm, counts_hbm, rows_ref, counts_ref, sem_i)
     m_ref[...] = g_ref[...] * (1.0 / features)
-    for copy in indices:
-        copy.wait()
 
     def tile(f):
         row = lax.div(f, 2)
@@ -379,26 +385,55 @@
             parts.append(y_ref[s, m % 2, a, b, lax.rem(z, QZ)])
         return jnp.concatenate(parts, axis=0)
 
-    for d in range(docs):
+    def product(d):
         parts = []
         for s in range(slots):
             part = tile(rows_ref[s, d])
             parts.append(jnp.where(s < counts_ref[d], part, jnp.zeros_like(part)))
         t_ref[d] = jnp.dot(bt_ref[d], jnp.concatenate(parts, axis=0), preferred_element_type=F32)
-    factor(m_ref, linv_ref, 16)
+
+    panels = width // PANEL
+
+    def between(panel):
+        if panel == 0:
+            for copy in indices:
+                copy.wait()
+        last = docs * (panel + 1) // panels
+        for d in range(docs * panel // panels, last):
+            product(d)
+
+    factor(m_ref, linv_ref, PANEL, between)
     inverse = linv_ref[...]
-    basis_ref[...] = lax.dot_general(
-        s_ref[...], inverse, (((1,), (1,)), ((), ())), precision=HIGHEST, preferred_element_type=F32
-    )
     high, low = split(inverse)
-    both = jnp.concatenate([high, high, low], axis=1)
+    left = jnp.concatenate([high, low], axis=0)
+    right = jnp.concatenate([high, jnp.zeros_like(low)], axis=0)
+    both = jnp.concatenate([left, right], axis=1)
+    copies = []
+
+    def put(src, dst):
+        copy = pltpu.make_async_copy(src, dst, sem_o.at[len(copies)])
+        copy.start()
+        copies.append(copy)
+
     for d in range(docs):
         t_high, t_low = split(t_ref[d])
         out = lax.dot_general(
-            jnp.concatenate([t_high, t_low, t_high], axis=1), both,
+            jnp.concatenate([t_high, t_low], axis=1), both,
             (((1,), (1,)), ((), ())), preferred_element_type=F32,
         )
-        factors_ref[d * width : (d + 1) * width, :] = out.astype(BF16)
+        rows = pl.ds(d * width, width)
+        f_ref[rows, :] = (out[:, :width] + out[:, width:]).astype(BF16)
+        if d % 4 == 3:
+            rows = pl.ds((d - 3) * width, 4 * width)
+            put(f_ref.at[rows], factors_ref.at[rows])
+        if d == 0:
+            b_ref[...] = lax.dot_general(
+                s_ref[...], inverse, (((1,), (1,)), ((), ())),
+                precision=HIGHEST, preferred_element_type=F32,
+            )
+            put(b_ref, basis_ref)
+    for copy in copies:
+        copy.wait()
 
 
 def vmem():
@@ -467,10 +502,11 @@
             jax.ShapeDtypeStruct((docs * width, columns), BF16),
         ),
         in_specs=[hbm(), hbm(), vmem(), vmem(), vmem(), vmem()],
-        out_specs=(vmem(), vmem()),
+        out_specs=(hbm(), hbm()),
         scratch_shapes=[
             pltpu.VMEM(square, F32), pltpu.VMEM(square, F32),
             pltpu.VMEM((docs,) + square, F32),
+            pltpu.VMEM((docs * width, columns), BF16), pltpu.VMEM(tail, F32), dma((docs // 4 + 1,)),
             pltpu.SMEM(rows.shape, jnp.int32), pltpu.SMEM(counts.shape, jnp.int32), dma((2,)),
         ],
         compiler_params=params(),

time: 55.9 us -> 54.6 us (0.977)
  Pallas kernels: 55.1 us -> 53.8 us
    pallas_call x1, Pallas kernels: 6.12 us -> 4.96 us  [body(): pl.pallas_call(tail_kernel, name='tail', out_shape=(jax.ShapeDtypeStruct(...]
where the time goes in v5:
time: 54.6 us; the launch traced here: 54.4 us
  Pallas kernels  53.8 us (99%)
  between operations  0.66 us (1%)
    pallas_call x1, Pallas kernels, body(): pl.pallas_call(exchange_kernel, name='exchange', out_shape=(jax.ShapeDtyp...  46.6 us
    pallas_call x1, Pallas kernels, body(): pl.pallas_call(tail_kernel, name='tail', out_shape=(jax.ShapeDtypeStruct(...  4.96 us
    pallas_call x1, Pallas kernels, body(): pl.pallas_call(terms_kernel, name='terms', out_shape=jax.ShapeDtypeStruct...  2.25 us

profile of v5, /device:TPU:1, one launch (start us, length us, event | category | flops | bytes accessed | tf_op | source)
XLA Modules:
  0.0 54.4 jit_solution(8934888563546536003)
XLA Ops:
  0.6 0.0 copy-start
  0.6 2.3 %terms.1 = f32[64,128,128]{2,1,0:T(8,128)S(1)} custom-call(s32[3,16]{1,0:T(4,128)} %bitcast.5, s32[16]{0:T(128)} %counts_hbm.3, bf16[16,3,128,128]{3,2,1,0:T(8,128)(2,1)} %blocks_ref.3, bf16[2048,128]{1,0:T(8,128)(2,1)} %sketch_ref.1), custom_call_target="tpu_custom_call" | custom-call | tf_op jit(solution)/shard_map/terms/pallas_call | solution.py:460
  2.9 0.0 copy-done
  2.9 46.6 %exchange.1 = (bf16[4,2,4,4,2,32,128]{6,5,4,3,2,1,0:T(8,128)(2,1)S(1)}, f32[32,128]{1,0:T(8,128)S(1)}, f32[128,128]{1,0:T(8,128)S(1)}, bf16[16,128,384]{2,1,0:T(8,128)(2,1)S(1)}) custom-call(f32[4,8,4,2,32,128]{5,4,3,2,1,0:T(8,128)S(1)} %bitcast.3, f32[64,128]{1,0:T(8,128)S(1)} %bitcast.4, bf16[16,3,128,128]{3,2,1,0:T(8,128)(2,1)} %blocks_ref.3), custom_call_target="tpu_custom_call" | custom-call | tf_op jit(solution)/shard_map/exchange/pallas_call | solution.py:475
  49.5 5.0 %tail.1 = (f32[32,128]{1,0:T(8,128)}, bf16[2048,128]{1,0:T(8,128)(2,1)}) custom-call(s32[3,16]{1,0:T(4,128)} %bitcast.6, s32[16]{0:T(128)} %counts_hbm.3, bf16[4,2,4,4,2,32,128]{6,5,4,3,2,1,0:T(8,128)(2,1)S(1)} %get-tuple-element.6.y_ref, bf16[16,128,384]{2,1,0:T(8,128)(2,1)S(1)} %get-tuple-element.7.bt_ref, f32[128,128]{1,0:T(8,128)S(1)} %get-tuple-element.8.g_ref, ...), custom_call_target="tpu_custom_call" | custom-call | tf_op jit(solution)/shard_map/tail/pallas_call | solution.py:497
Async XLA Ops:
  0.6 2.3 %copy-start = (f32[8192]{0:T(1024)S(1)}, f32[8192]{0:T(1024)}, u32[]{:S(2)}) copy-start(f32[8192]{0:T(1024)} %param.9) | copy-start | bytes 98308

commit v6 on v5

--- a/solution.py
+++ b/solution.py
@@ -31,7 +31,7 @@
     held, docs_held, sems, rows_ref, counts_ref, sem_i,
 ):
     docs, slots, width = held.shape[:3]
-    step = 4
+    step = 8
     indices = scalars(rows_hbm, counts_hbm, rows_ref, counts_ref, sem_i)
     copies = []
     for i in range(docs // step):
@@ -149,8 +149,7 @@
             scaled, part, (((0,), (0,)), ((), ())), preferred_element_type=F32
         )
 
-    order = [(s, k) for s0 in (0, 2) for k in (2, 1, 3, 0) for s in (s0, s0 + 1)]
-    for s, k in order:
+    for s, k in [(s, k) for s in streams for k in range(4)]:
         def fill(b, carry, s=s, k=k):
             for j in range(QZ):
                 cs[s * 4 + k, b, j] = p_ref[piece(s, k, b, j, 1 - c)].astype(BF16)
@@ -164,13 +163,12 @@
     pl.semaphore_wait(barrier, len(greet))
 
     first, second, third = {}, {}, {}
-    for s, k in order:
-        n = s * 4 + k
-        first[s, k] = send(cs.at[n], cr.at[n], sem0, n, partner)
-    for s, k in order:
-        first[s, k].wait_recv()
-        if k == 0:
-            continue
+    for s in streams:
+        four = pl.ds(s * 4, 4)
+        first[s] = send(cs.at[four], cr.at[four], sem0, s, partner)
+    for s, k in [(s, k) for s in streams for k in (2, 1, 3)]:
+        if k == 2:
+            first[s].wait_recv()
         n = s * 3 + k - 1
 
         def add(b, carry, s=s, k=k, n=n):
@@ -237,6 +235,8 @@
     mine_a, mine_b = x + odd * (y - x), y + odd * (x - y)
     y_ref[mine_s, c, mine_a, mine_b, lax.rem(z, QZ)] = (summed * w).astype(BF16)
     mine = y_ref.at[mine_s, c, mine_a, mine_b, lax.rem(z, QZ)]
+    old = list(started)
+    started.clear()
     for k in (4, 3, 5, 2, 6, 1, 7):
         copy = copy_to(mine, mine, sem_gz.at[0, k], sem_gz.at[1, z], z_peer[k])
         copy.start()
@@ -246,6 +246,10 @@
     load.wait()
     turn_tiles(0, 4)
     g_ref[...] = jnp.zeros_like(g_ref)
+    for copy in old:
+        copy.wait_send()
+    for k in range(1, NZ):
+        arrival(k).wait_send()
 
     def pair(part):
         paired.append(send(part, part, sem_p, len(paired), partner))
@@ -269,27 +273,29 @@
         part = y_ref.at[s, c, a_at[s]]
         for k in (2, 1, 3):
             ga[s, k] = send(part, part, sem_ga, s * 3 + k - 1, a_peer[s][k])
-        pair(part)
+    last = list(ga.values())
+    for copy in started[: -len(last)]:
+        copy.wait_send()
+
     def add_partner(s):
-        for copy in [paired[s]] + paired[4 + 3 * s : 7 + 3 * s]:
-            copy.wait_recv()
+        paired[s].wait_recv()
         add_gram(s, 1 - c)
 
     for s in streams:
         for k in (1, 3, 2):
             ga[s, k].wait_recv()
-            pair(y_ref.at[s, c, shift(a_at[s], 4 - k, 4)])
+        pair(y_ref.at[s, c])
         if s > 0:
             add_gram(s - 1, c)
         if s > 1:
             add_partner(s - 2)
     add_gram(streams[-1], c)
+    for copy in last:
+        copy.wait_send()
     for s in streams[-2:]:
         add_partner(s)
-    for copy in started:
+    for copy in paired:
         copy.wait_send()
-    for k in range(1, NZ):
-        arrival(k).wait_send()
 
 
 def split(a):
@@ -464,7 +470,7 @@
         in_specs=[hbm()] * 4,
         out_specs=vmem(),
         scratch_shapes=[
-            pltpu.VMEM(blocks.shape, BF16), pltpu.VMEM(sketch.shape, BF16), dma((2, 4)),
+            pltpu.VMEM(blocks.shape, BF16), pltpu.VMEM(sketch.shape, BF16), dma((2, 2)),
             pltpu.SMEM(rows.shape, jnp.int32), pltpu.SMEM(counts.shape, jnp.int32), dma((2,)),
         ],
         compiler_params=params(),
@@ -489,8 +495,8 @@
             pltpu.VMEM((12, QZ) + tail, BF16), pltpu.VMEM((12, QZ) + tail, BF16),
             pltpu.VMEM((NZ,) + tail, F32), pltpu.VMEM((NZ,) + tail, F32),
             pltpu.VMEM(square, F32),
-            dma((2, 16)), dma((2, 12)), dma((2, 12)), dma((2, NZ)),
-            dma((2, NZ)), dma((2, 12)), dma((2, 12)), dma((2, 16)),
+            dma((2, 4)), dma((2, 12)), dma((2, 12)), dma((2, NZ)),
+            dma((2, NZ)), dma((2, 12)), dma((2, 12)), dma((2, 4)),
         ],
         compiler_params=params(collective_id=0, has_side_effects=True),
     )(terms.reshape(grid), w, blocks)

time: 54.6 us -> 53.7 us (0.984)
  Pallas kernels: 53.8 us -> 52.9 us
    pallas_call x1, Pallas kernels: 46.6 us -> 45.8 us  [body(): pl.pallas_call(exchange_kernel, name='exchange', out_shape=(jax.ShapeDtyp...]
where the time goes in v6:
time: 53.7 us; the launch traced here: 53.5 us
  Pallas kernels  52.9 us (99%)
  between operations  0.66 us (1%)
    pallas_call x1, Pallas kernels, body(): pl.pallas_call(exchange_kernel, name='exchange', out_shape=(jax.ShapeDtyp...  45.8 us
    pallas_call x1, Pallas kernels, body(): pl.pallas_call(tail_kernel, name='tail', out_shape=(jax.ShapeDtypeStruct(...  4.97 us
    pallas_call x1, Pallas kernels, body(): pl.pallas_call(terms_kernel, name='terms', out_shape=jax.ShapeDtypeStruct...  2.04 us

profile of v6, /device:TPU:1, one launch (start us, length us, event | category | flops | bytes accessed | tf_op | source)
XLA Modules:
  0.0 53.5 jit_solution(18374375887729732191)
XLA Ops:
  0.6 0.0 copy-start
  0.6 2.0 %terms.1 = f32[64,128,128]{2,1,0:T(8,128)S(1)} custom-call(s32[3,16]{1,0:T(4,128)} %bitcast.5, s32[16]{0:T(128)} %counts_hbm.3, bf16[16,3,128,128]{3,2,1,0:T(8,128)(2,1)} %blocks_ref.3, bf16[2048,128]{1,0:T(8,128)(2,1)} %sketch_ref.1), custom_call_target="tpu_custom_call" | custom-call | tf_op jit(solution)/shard_map/terms/pallas_call | solution.py:466
  2.7 0.0 copy-done
  2.7 45.8 %exchange.1 = (bf16[4,2,4,4,2,32,128]{6,5,4,3,2,1,0:T(8,128)(2,1)S(1)}, f32[32,128]{1,0:T(8,128)S(1)}, f32[128,128]{1,0:T(8,128)S(1)}, bf16[16,128,384]{2,1,0:T(8,128)(2,1)S(1)}) custom-call(f32[4,8,4,2,32,128]{5,4,3,2,1,0:T(8,128)S(1)} %bitcast.3, f32[64,128]{1,0:T(8,128)S(1)} %bitcast.4, bf16[16,3,128,128]{3,2,1,0:T(8,128)(2,1)} %blocks_ref.3), custom_call_target="tpu_custom_call" | custom-call | tf_op jit(solution)/shard_map/exchange/pallas_call | solution.py:481
  48.6 5.0 %tail.1 = (f32[32,128]{1,0:T(8,128)}, bf16[2048,128]{1,0:T(8,128)(2,1)}) custom-call(s32[3,16]{1,0:T(4,128)} %bitcast.6, s32[16]{0:T(128)} %counts_hbm.3, bf16[4,2,4,4,2,32,128]{6,5,4,3,2,1,0:T(8,128)(2,1)S(1)} %get-tuple-element.6.y_ref, bf16[16,128,384]{2,1,0:T(8,128)(2,1)S(1)} %get-tuple-element.7.bt_ref, f32[128,128]{1,0:T(8,128)S(1)} %get-tuple-element.8.g_ref, ...), custom_call_target="tpu_custom_call" | custom-call | tf_op jit(solution)/shard_map/tail/pallas_call | solution.py:503
Async XLA Ops:
  0.6 2.1 %copy-start = (f32[8192]{0:T(1024)S(1)}, f32[8192]{0:T(1024)}, u32[]{:S(2)}) copy-start(f32[8192]{0:T(1024)} %param.9) | copy-start | bytes 98308

commit v7 on v6

--- a/solution.py
+++ b/solution.py
@@ -171,16 +171,12 @@
             first[s].wait_recv()
         n = s * 3 + k - 1
 
-        def add(b, carry, s=s, k=k, n=n):
+        for b in range(4):
             for j in range(QZ):
                 total = p_ref[piece(s, k, b, j, c)] + cr[s * 4 + k, b, j].astype(F32)
                 xs[n, b, j] = total.astype(BF16)
-            return carry
-
-        lax.fori_loop(0, 4, add, 0)
         second[s, k] = send(xs.at[n], xr.at[n], sem_a, n, a_peer[s][k])
 
-    inverse_weights(0, 2)
     for s in streams:
         for k in (1, 3, 2):
             second[s, k].wait_recv()
@@ -207,6 +203,7 @@
         here = shift(z, k, NZ)
         return copy_to(zs.at[here], zr.at[here], sem_z.at[0, here], sem_z.at[1, here], z_peer[k])
 
+    inverse_weights(0, 2)
     for s in streams:
         for k in (1, 3, 2):
             third[s, k].wait_recv()

time: 53.7 us -> 53.5 us (level)
  no operation moved by 1% of the time
where the time goes in v7:
time: 53.5 us; the launch traced here: 53.4 us
  Pallas kernels  52.7 us (99%)
  between operations  0.66 us (1%)
    pallas_call x1, Pallas kernels, body(): pl.pallas_call(exchange_kernel, name='exchange', out_shape=(jax.ShapeDtyp...  45.7 us
    pallas_call x1, Pallas kernels, body(): pl.pallas_call(tail_kernel, name='tail', out_shape=(jax.ShapeDtypeStruct(...  4.97 us
    pallas_call x1, Pallas kernels, body(): pl.pallas_call(terms_kernel, name='terms', out_shape=jax.ShapeDtypeStruct...  2.04 us

profile of v7, /device:TPU:1, one launch (start us, length us, event | category | flops | bytes accessed | tf_op | source)
XLA Modules:
  0.0 53.4 jit_solution(12690299097649009105)
XLA Ops:
  0.6 0.0 copy-start
  0.6 2.0 %terms.1 = f32[64,128,128]{2,1,0:T(8,128)S(1)} custom-call(s32[3,16]{1,0:T(4,128)} %bitcast.5, s32[16]{0:T(128)} %counts_hbm.3, bf16[16,3,128,128]{3,2,1,0:T(8,128)(2,1)} %blocks_ref.3, bf16[2048,128]{1,0:T(8,128)(2,1)} %sketch_ref.1), custom_call_target="tpu_custom_call" | custom-call | tf_op jit(solution)/shard_map/terms/pallas_call | solution.py:463
  2.7 0.0 copy-done
  2.7 45.7 %exchange.1 = (bf16[4,2,4,4,2,32,128]{6,5,4,3,2,1,0:T(8,128)(2,1)S(1)}, f32[32,128]{1,0:T(8,128)S(1)}, f32[128,128]{1,0:T(8,128)S(1)}, bf16[16,128,384]{2,1,0:T(8,128)(2,1)S(1)}) custom-call(f32[4,8,4,2,32,128]{5,4,3,2,1,0:T(8,128)S(1)} %bitcast.3, f32[64,128]{1,0:T(8,128)S(1)} %bitcast.4, bf16[16,3,128,128]{3,2,1,0:T(8,128)(2,1)} %blocks_ref.3), custom_call_target="tpu_custom_call" | custom-call | tf_op jit(solution)/shard_map/exchange/pallas_call | solution.py:478
  48.4 5.0 %tail.1 = (f32[32,128]{1,0:T(8,128)}, bf16[2048,128]{1,0:T(8,128)(2,1)}) custom-call(s32[3,16]{1,0:T(4,128)} %bitcast.6, s32[16]{0:T(128)} %counts_hbm.3, bf16[4,2,4,4,2,32,128]{6,5,4,3,2,1,0:T(8,128)(2,1)S(1)} %get-tuple-element.6.y_ref, bf16[16,128,384]{2,1,0:T(8,128)(2,1)S(1)} %get-tuple-element.7.bt_ref, f32[128,128]{1,0:T(8,128)S(1)} %get-tuple-element.8.g_ref, ...), custom_call_target="tpu_custom_call" | custom-call | tf_op jit(solution)/shard_map/tail/pallas_call | solution.py:500
Async XLA Ops:
  0.6 2.1 %copy-start = (f32[8192]{0:T(1024)S(1)}, f32[8192]{0:T(1024)}, u32[]{:S(2)}) copy-start(f32[8192]{0:T(1024)} %param.9) | copy-start | bytes 98308
